TPU v7x, 32 devices: a whole 2x2x4 slice. The times are simulated.
32 devices in a mesh: tm: 16 (over z, x, core), space: 2 (over y).
Axes of the slice: x: 2, y: 2, z: 4, core: 2. Of those that a mesh axis runs over, the one named last changes fastest.
Arguments:
- initial: float32 [16, 64, 128], P('space'), may hold values from -6 to 6
- forcing: bfloat16 [64, 16, 64, 128], P('tm', 'space'), may hold values from -4 to 4
- brick_blocks: bfloat16 [16, 64, 448], P('space'), may hold values from -1 to 1
- neighbours: int32 [16, 6], P('space'), may hold values from 0 to 15, as said below
- coarse_modes: float32 [8, 64], replicated, may hold values from -0.75 to 0.75
- coarse_blocks: float32 [16, 8, 8], P('space'), may hold values from -1 to 1.2
Outputs:
- solution: float32 [64, 16, 64, 128], P('tm', 'space')
- last_defect: float32 [16, 16, 64, 128], P('tm', 'space')
Inputs may be any that keep to these rules, and one draw needn't show every extreme that they name: `neighbours`: each brick's 6 slots name distinct bricks other than itself, in a random slot order, each at most 4 positions away along the periodic brick order; every brick names the bricks directly before and after it and one brick exactly 4 away.
All inputs are finite; a program needn't handle non-finite values.
Results may differ from a plain program's by a relative error of at most 0.014.
Values may be sent and summed in bfloat16 or wider, within the bound.
No kernel may reach another device: no remote copies, remote signals or barrier semaphores. Data moves between devices by JAX's collectives and lax.ppermute only.
A program may use at most 64 MiB of HBM per device.

v0:
```python
import jax
import jax.numpy as jnp
from jax import lax
from jax.sharding import PartitionSpec as P

BRICK = 64
REACH = 4
Q = 8
SWEEPS = 3
STEPS = 4
ITERS = 2


highest = lax.Precision.HIGHEST


def extended(block, sides, width):
    for axis, dim in sides:
        count = lax.axis_size(axis)
        forward = [(i, i + 1) for i in range(count - 1)]
        forward.append((count - 1, 0))
        backward = [(target, source) for source, target in forward]
        low = lax.ppermute(
            lax.slice_in_dim(block, block.shape[dim] - width, None, axis=dim), axis, forward
        )
        high = lax.ppermute(lax.slice_in_dim(block, 0, width, axis=dim), axis, backward)
        block = jnp.concatenate([low, block, high], axis=dim)
    return block


def carried_in(part, axis, combine, identity):
    place = lax.axis_index(axis)
    gathered = jax.tree.map(lambda a: lax.all_gather(a, axis), part)
    state = jax.tree.map(lambda a, e: jnp.zeros_like(a) + jnp.asarray(e, a.dtype), part, identity)

    def one(turn, state):
        return combine(
            state, jax.tree.map(lambda a: lax.dynamic_index_in_dim(a, turn, 0, False), gathered)
        )

    return lax.fori_loop(0, place, one, state)


def from_behind(block, axis, distance):
    devices = range(lax.axis_size(axis))
    route = [(i - distance, i) for i in devices if i - distance in devices]
    return lax.ppermute(block, axis, route)


def apply_inverse(diag_blocks, values):
    return jnp.einsum(
        "bij,bje->bie", diag_blocks, values.astype(jnp.bfloat16), preferred_element_type=jnp.float32
    )


def coupling(off_blocks, source, positions):
    picked = jnp.take(source, positions, axis=0)
    merged = picked.reshape(
        positions.shape[0], positions.shape[1] * source.shape[1], source.shape[2]
    )
    return jnp.einsum("bim,bme->bie", off_blocks, merged, preferred_element_type=jnp.float32)


def wrapped_offsets(indices, first_row, bricks_all):
    row_ids = jnp.arange(indices.shape[0], dtype=jnp.int32)
    position = jnp.mod(first_row + row_ids, bricks_all)
    return jnp.mod(indices - position[:, None] + REACH, bricks_all) - REACH


def body(initial, forcing, brick_blocks, neighbours, coarse_modes, coarse_blocks):
    bricks_here = initial.shape[0]
    bricks_all = bricks_here * lax.axis_size("space")
    first_brick = lax.axis_index("space") * bricks_here
    slice_index = lax.axis_index("tm")
    own_shifts = wrapped_offsets(neighbours, first_brick, bricks_all)
    where_from = jnp.arange(bricks_here, dtype=jnp.int32)[:, None] + REACH + own_shifts
    diagonal = brick_blocks[:, :, :BRICK]
    off_blocks = brick_blocks[:, :, BRICK:]

    def propagate(values):
        iterate = apply_inverse(diagonal, values)
        for sweep_index in range(1, SWEEPS):
            rimmed = extended(iterate.astype(jnp.bfloat16), (("space", 0),), REACH)
            iterate = apply_inverse(diagonal, values - coupling(off_blocks, rimmed, where_from))
        return iterate

    is_first = slice_index == 0
    slice_starts = jnp.where(is_first, initial, jnp.zeros_like(initial))
    slice_ends = jnp.zeros_like(initial)
    identity = jnp.broadcast_to(jnp.eye(Q, dtype=jnp.float32), coarse_blocks.shape)
    nothing = jnp.zeros((bricks_here, Q, initial.shape[2]), jnp.float32)

    def compose(earlier, later):
        matrix = jnp.einsum("bpq,bqr->bpr", later[0], earlier[0], precision=highest)
        offset = jnp.einsum("bpq,bqe->bpe", later[0], earlier[1], precision=highest) + later[1]
        return (matrix, offset)

    defect = slice_ends
    for count_iter in range(ITERS):
        current = slice_starts
        for substep in range(STEPS - 1):
            current = propagate(current) + forcing[substep].astype(jnp.float32)
        defect = propagate(current) + forcing[STEPS - 1].astype(jnp.float32) - slice_ends
        restricted = jnp.einsum("qc,bce->bqe", coarse_modes, defect, precision=highest)
        prefix = carried_in((coarse_blocks, restricted), "tm", compose, (identity, nothing))
        before = prefix[1]
        corrected = (
            jnp.einsum("bpq,bqe->bpe", coarse_blocks, before, precision=highest) + restricted
        )
        slice_ends = slice_ends + jnp.einsum(
            "qc,bqe->bce", coarse_modes, corrected, precision=highest
        )
        shifted = from_behind(slice_ends.astype(jnp.bfloat16), "tm", 1).astype(slice_ends.dtype)
        slice_starts = jnp.where(is_first, initial, shifted)
    outputs = []
    current = slice_starts
    for substep in range(STEPS - 1):
        current = propagate(current) + forcing[substep].astype(jnp.float32)
        outputs.append(current)
    outputs.append(slice_ends)
    return (jnp.stack(outputs, 0), defect[None])


def solution(mesh):
    placed = (
        P("space", None, None),
        P("tm", "space", None, None),
        P("space", None, None),
        P("space", None),
        P(),
        P("space", None, None),
    )
    return jax.shard_map(
        body,
        mesh=mesh,
        in_specs=placed,
        out_specs=(P("tm", "space", None, None), P("tm", "space", None, None)),
        check_vma=False,
    )
```

profile of v0, /device:TPU:26, one launch (start us, length us, event | category | flops | bytes accessed | tf_op | source)
XLA Modules:
  0.0 257.8 jit_solution(4958261347449941342)
XLA Ops:
  0.7 1.1 fusion.64
  1.8 1.6 collective-permute-start.1
  4.7 2.0 collective-permute-done.1
  11.0 1.1 collective-permute-start.2
  12.0 2.2 collective-permute-done.3
  17.7 1.1 collective-permute-start.5
  19.8 2.2 collective-permute-done.5
  22.0 1.1 collective-permute-done.4
  25.5 1.1 collective-permute-start.6
  26.5 2.2 collective-permute-done.7
  28.8 1.7 collective-permute-done.6
  32.0 1.1 collective-permute-start.9
  34.1 2.9 %collective-permute-done.9 = bf16[4,64,128]{2,1,0:T(8,128)(2,1)S(1)} collective-permute-done((bf16[4,64,128]{2,1,0:T(8,128)(2,1)S(1)}, bf16[4,64,128]{2,1,0:T(8,128)(2,1)S(1)}, u32[]{:S(2)}, u32[]{:S(2)}) %collective-permute-start.9) | collective-permute-done | bytes 65568 | tf_op jit(solution)/shard_map/ppermute | solution.py:26
  39.0 1.0 collective-permute-start.11
  41.1 2.2 collective-permute-done.11
  45.9 1.1 collective-permute-start.13
  48.0 2.2 collective-permute-done.13
  50.2 1.0 collective-permute-done.12
  52.6 1.0 collective-permute-start.15
  53.7 1.0 collective-permute-start.14
  54.7 19.1 %all-gather = f32[128,8,8]{2,1,0:T(8,128)} all-gather(f32[8,8,8]{2,1,0:T(8,128)S(1)} %copy-done.7), channel_id=2, replica_groups=mesh['tm'=16,'space'=2] {'tm'}, dimensions={0}, use_global_device_ids=true | all-gather | bytes 34816 | tf_op jit(solution)/shard_map/all_gather | solution.py:33
  75.5 21.3 %all-gather.1 = f32[128,8,128]{2,1,0:T(8,128)S(1)} all-gather(f32[8,8,128]{2,1,0:T(8,128)S(1)} %convolution_bitcast_fusion.38), channel_id=3, replica_groups=mesh['tm'=16,'space'=2] {'tm'}, dimensions={0}, use_global_device_ids=true | all-gather | bytes 557056 | tf_op jit(solution)/shard_map/all_gather | solution.py:33
  96.8 13.8 %while.24 = (s32[]{:T(128)}, f32[8,8,128]{2,1,0:T(8,128)S(1)}, s32[]{:T(128)}, f32[16,8,8,8]{3,2,1,0:T(8,128)}, f32[16,8,8,128]{3,2,1,0:T(8,128)S(1)}, /*index=5*/s32[]{:T(128)}, s32[]{:T(128)}, s32[]{:T(128)}) while((s32[]{:T(128)}, f32[8,8,128]{2,1,0:T(8,128)S(1)}, s32[]{:T(128)}, f32[16,8,8,8]{3,2,1,0:T(8,128)}, ...), condition=%wide.region_1.3_spmd, body=%wide.region_0.2_spmd.sunk | while | flops 794629 | bytes 197759 | solution.py:41
  110.9 1.1 fusion.216
  112.0 3.4 %collective-permute-start.16 = (bf16[8,64,128]{2,1,0:T(8,128)(2,1)S(1)}, bf16[8,64,128]{2,1,0:T(8,128)(2,1)S(1)}, u32[]{:S(2)}, u32[]{:S(2)}) collective-permute-start(bf16[8,64,128]{2,1,0:T(8,128)(2,1)S(1)} %get-tuple-element.159), channel_id=1, source_target_pairs={{0,2},{2,4},{4,6},{6,8},{8,10},{10,12},{12,14},{14,16},{16,18},{18... | collective-permute-start | bytes 393224 | tf_op jit(solution)/shard_map/ppermute | solution.py:47
  115.4 2.8 %collective-permute-done.16 = bf16[8,64,128]{2,1,0:T(8,128)(2,1)S(1)} collective-permute-done((bf16[8,64,128]{2,1,0:T(8,128)(2,1)S(1)}, bf16[8,64,128]{2,1,0:T(8,128)(2,1)S(1)}, u32[]{:S(2)}, u32[]{:S(2)}) %collective-permute-start.16) | collective-permute-done | bytes 131104 | tf_op jit(solution)/shard_map/ppermute | solution.py:47
  119.5 1.0 collective-permute-start.17
  120.5 2.2 collective-permute-done.18
  125.1 1.1 collective-permute-start.20
  127.2 2.2 collective-permute-done.20
  129.5 1.4 collective-permute-done.19
  133.4 1.0 collective-permute-start.21
  134.5 2.9 %collective-permute-done.22 = bf16[4,64,128]{2,1,0:T(8,128)(2,1)S(1)} collective-permute-done((bf16[4,64,128]{2,1,0:T(8,128)(2,1)S(1)}, bf16[4,64,128]{2,1,0:T(8,128)(2,1)S(1)}, u32[]{:S(2)}, u32[]{:S(2)}) %collective-permute-start.22) | collective-permute-done | bytes 65568 | tf_op jit(solution)/shard_map/ppermute | solution.py:26
  137.4 1.1 collective-permute-done.21
  141.0 1.0 collective-permute-start.23
  142.0 2.7 %collective-permute-done.24 = bf16[4,64,128]{2,1,0:T(8,128)(2,1)S(1)} collective-permute-done((bf16[4,64,128]{2,1,0:T(8,128)(2,1)S(1)}, bf16[4,64,128]{2,1,0:T(8,128)(2,1)S(1)}, u32[]{:S(2)}, u32[]{:S(2)}) %collective-permute-start.24) | collective-permute-done | bytes 65568 | tf_op jit(solution)/shard_map/ppermute | solution.py:26
  147.0 1.1 collective-permute-start.26
  149.1 2.2 collective-permute-done.26
  153.7 1.0 collective-permute-start.28
  155.8 2.2 collective-permute-done.28
  160.6 1.1 collective-permute-start.30
  162.7 2.2 collective-permute-done.30
  167.3 1.0 collective-permute-start.32
  169.4 2.2 collective-permute-done.32
  175.0 17.7 %all-gather.2 = f32[128,8,128]{2,1,0:T(8,128)S(1)} all-gather(f32[8,8,128]{2,1,0:T(8,128)S(1)} %convolution_bitcast_fusion.36), channel_id=4, replica_groups=mesh['tm'=16,'space'=2] {'tm'}, dimensions={0}, use_global_device_ids=true | all-gather | bytes 557056 | tf_op jit(solution)/shard_map/all_gather | solution.py:33
  192.8 13.9 %while.25 = (s32[]{:T(128)}, f32[8,8,128]{2,1,0:T(8,128)S(1)}, s32[]{:T(128)}, f32[16,8,8,8]{3,2,1,0:T(8,128)}, f32[16,8,8,128]{3,2,1,0:T(8,128)S(1)}, /*index=5*/s32[]{:T(128)}, s32[]{:T(128)}, s32[]{:T(128)}) while((s32[]{:T(128)}, f32[8,8,128]{2,1,0:T(8,128)S(1)}, s32[]{:T(128)}, f32[16,8,8,8]{3,2,1,0:T(8,128)}, ...), condition=%wide.region_3.5_spmd, body=%wide.region_2.4_spmd.sunk | while | flops 794629 | bytes 197759 | solution.py:41
  206.8 1.1 fusion.217
  208.0 3.3 %collective-permute-start.33 = (bf16[8,64,128]{2,1,0:T(8,128)(2,1)S(1)}, bf16[8,64,128]{2,1,0:T(8,128)(2,1)S(1)}, u32[]{:S(2)}, u32[]{:S(2)}) collective-permute-start(bf16[8,64,128]{2,1,0:T(8,128)(2,1)S(1)} %get-tuple-element.161), channel_id=1, source_target_pairs={{0,2},{2,4},{4,6},{6,8},{8,10},{10,12},{12,14},{14,16},{16,18},{18... | collective-permute-start | bytes 393224 | tf_op jit(solution)/shard_map/ppermute | solution.py:47
  211.2 3.0 %collective-permute-done.33 = bf16[8,64,128]{2,1,0:T(8,128)(2,1)S(1)} collective-permute-done((bf16[8,64,128]{2,1,0:T(8,128)(2,1)S(1)}, bf16[8,64,128]{2,1,0:T(8,128)(2,1)S(1)}, u32[]{:S(2)}, u32[]{:S(2)}) %collective-permute-start.33) | collective-permute-done | bytes 131104 | tf_op jit(solution)/shard_map/ppermute | solution.py:47
  214.4 1.1 collective-permute-start.35
  216.5 2.2 collective-permute-done.35
  218.8 1.0 collective-permute-done.34
  222.2 1.0 collective-permute-start.36
  223.3 2.2 collective-permute-done.37
  225.5 1.5 collective-permute-done.36
  228.6 1.1 collective-permute-start.39
  230.7 2.9 %collective-permute-done.39 = bf16[4,64,128]{2,1,0:T(8,128)(2,1)S(1)} collective-permute-done((bf16[4,64,128]{2,1,0:T(8,128)(2,1)S(1)}, bf16[4,64,128]{2,1,0:T(8,128)(2,1)S(1)}, u32[]{:S(2)}, u32[]{:S(2)}) %collective-permute-start.39) | collective-permute-done | bytes 65568 | tf_op jit(solution)/shard_map/ppermute | solution.py:26
  235.9 1.1 collective-permute-start.41
  238.0 2.6 collective-permute-done.41
  243.9 1.0 collective-permute-start.42
  244.9 2.2 collective-permute-done.43
  249.5 1.1 collective-permute-start.45
  251.6 2.2 collective-permute-done.45
  253.8 1.0 collective-permute-done.44
  (241 shorter events, 96.4 us)
Async XLA Ops:
  0.6 74.6 %copy-start = (f32[8,64]{1,0:T(8,128)S(1)}, f32[8,64]{1,0:T(8,128)}, u32[]{:S(2)}) copy-start(f32[8,64]{1,0:T(8,128)} %param.16) | copy-start | bytes 6148
  1.8 4.9 %collective-permute-start.1 = (bf16[4,64,128]{2,1,0:T(8,128)(2,1)S(1)}, bf16[4,64,128]{2,1,0:T(8,128)(2,1)S(1)}, u32[]{:S(2)}, u32[]{:S(2)}) collective-permute-start(bf16[4,64,128]{2,1,0:T(8,128)(2,1)S(1)} %get-tuple-element.158), channel_id=1, source_target_pairs={{1,0},{0,1},{3,2},{2,3},{5,4},{4,5},{7,6},{6,7},{9,8},{8,9},{11,10... | collective-permute-start | bytes 196616 | tf_op jit(solution)/shard_map/ppermute | solution.py:26
  3.3 4.3 %collective-permute-start = (bf16[4,64,128]{2,1,0:T(8,128)(2,1)S(1)}, bf16[4,64,128]{2,1,0:T(8,128)(2,1)S(1)}, u32[]{:S(2)}, u32[]{:S(2)}) collective-permute-start(bf16[4,64,128]{2,1,0:T(8,128)(2,1)S(1)} %get-tuple-element.157), channel_id=1, source_target_pairs={{0,1},{1,0},{2,3},{3,2},{4,5},{5,4},{6,7},{7,6},{8,9},{9,8},{10,11... | collective-permute-start | bytes 196616 | tf_op jit(solution)/shard_map/ppermute | solution.py:23
  3.8 0.7 copy-start.8
  8.3 1.0 copy-start.1
  8.4 1.1 copy-start.2
  9.9 4.3 %collective-permute-start.3 = (bf16[4,64,128]{2,1,0:T(8,128)(2,1)S(1)}, bf16[4,64,128]{2,1,0:T(8,128)(2,1)S(1)}, u32[]{:S(2)}, u32[]{:S(2)}) collective-permute-start(bf16[4,64,128]{2,1,0:T(8,128)(2,1)S(1)} %get-tuple-element.156), channel_id=1, source_target_pairs={{1,0},{0,1},{3,2},{2,3},{5,4},{4,5},{7,6},{6,7},{9,8},{8,9},{11,10... | collective-permute-start | bytes 196616 | tf_op jit(solution)/shard_map/ppermute | solution.py:26
  11.0 4.3 %collective-permute-start.2 = (bf16[4,64,128]{2,1,0:T(8,128)(2,1)S(1)}, bf16[4,64,128]{2,1,0:T(8,128)(2,1)S(1)}, u32[]{:S(2)}, u32[]{:S(2)}) collective-permute-start(bf16[4,64,128]{2,1,0:T(8,128)(2,1)S(1)} %get-tuple-element.155), channel_id=1, source_target_pairs={{0,1},{1,0},{2,3},{3,2},{4,5},{5,4},{6,7},{7,6},{8,9},{9,8},{10,11... | collective-permute-start | bytes 196616 | tf_op jit(solution)/shard_map/ppermute | solution.py:23
  16.0 1.0 copy-start.3
  17.7 4.3 %collective-permute-start.5 = (bf16[4,64,128]{2,1,0:T(8,128)(2,1)S(1)}, bf16[4,64,128]{2,1,0:T(8,128)(2,1)S(1)}, u32[]{:S(2)}, u32[]{:S(2)}) collective-permute-start(bf16[4,64,128]{2,1,0:T(8,128)(2,1)S(1)} %get-tuple-element.154), channel_id=1, source_target_pairs={{1,0},{0,1},{3,2},{2,3},{5,4},{4,5},{7,6},{6,7},{9,8},{8,9},{11,10... | collective-permute-start | bytes 196616 | tf_op jit(solution)/shard_map/ppermute | solution.py:26
  18.8 4.3 %collective-permute-start.4 = (bf16[4,64,128]{2,1,0:T(8,128)(2,1)S(1)}, bf16[4,64,128]{2,1,0:T(8,128)(2,1)S(1)}, u32[]{:S(2)}, u32[]{:S(2)}) collective-permute-start(bf16[4,64,128]{2,1,0:T(8,128)(2,1)S(1)} %get-tuple-element.153), channel_id=1, source_target_pairs={{0,1},{1,0},{2,3},{3,2},{4,5},{5,4},{6,7},{7,6},{8,9},{9,8},{10,11... | collective-permute-start | bytes 196616 | tf_op jit(solution)/shard_map/ppermute | solution.py:23
  24.4 4.3 %collective-permute-start.7 = (bf16[4,64,128]{2,1,0:T(8,128)(2,1)S(1)}, bf16[4,64,128]{2,1,0:T(8,128)(2,1)S(1)}, u32[]{:S(2)}, u32[]{:S(2)}) collective-permute-start(bf16[4,64,128]{2,1,0:T(8,128)(2,1)S(1)} %get-tuple-element.152), channel_id=1, source_target_pairs={{1,0},{0,1},{3,2},{2,3},{5,4},{4,5},{7,6},{6,7},{9,8},{8,9},{11,10... | collective-permute-start | bytes 196616 | tf_op jit(solution)/shard_map/ppermute | solution.py:26
  25.5 5.0 %collective-permute-start.6 = (bf16[4,64,128]{2,1,0:T(8,128)(2,1)S(1)}, bf16[4,64,128]{2,1,0:T(8,128)(2,1)S(1)}, u32[]{:S(2)}, u32[]{:S(2)}) collective-permute-start(bf16[4,64,128]{2,1,0:T(8,128)(2,1)S(1)} %get-tuple-element.151), channel_id=1, source_target_pairs={{0,1},{1,0},{2,3},{3,2},{4,5},{5,4},{6,7},{7,6},{8,9},{9,8},{10,11... | collective-permute-start | bytes 196616 | tf_op jit(solution)/shard_map/ppermute | solution.py:23
  32.0 5.0 %collective-permute-start.9 = (bf16[4,64,128]{2,1,0:T(8,128)(2,1)S(1)}, bf16[4,64,128]{2,1,0:T(8,128)(2,1)S(1)}, u32[]{:S(2)}, u32[]{:S(2)}) collective-permute-start(bf16[4,64,128]{2,1,0:T(8,128)(2,1)S(1)} %get-tuple-element.150), channel_id=1, source_target_pairs={{1,0},{0,1},{3,2},{2,3},{5,4},{4,5},{7,6},{6,7},{9,8},{8,9},{11,10... | collective-permute-start | bytes 196616 | tf_op jit(solution)/shard_map/ppermute | solution.py:26
  33.1 4.6 %collective-permute-start.8 = (bf16[4,64,128]{2,1,0:T(8,128)(2,1)S(1)}, bf16[4,64,128]{2,1,0:T(8,128)(2,1)S(1)}, u32[]{:S(2)}, u32[]{:S(2)}) collective-permute-start(bf16[4,64,128]{2,1,0:T(8,128)(2,1)S(1)} %get-tuple-element.149), channel_id=1, source_target_pairs={{0,1},{1,0},{2,3},{3,2},{4,5},{5,4},{6,7},{7,6},{8,9},{9,8},{10,11... | collective-permute-start | bytes 196616 | tf_op jit(solution)/shard_map/ppermute | solution.py:23
  39.0 4.3 %collective-permute-start.11 = (bf16[4,64,128]{2,1,0:T(8,128)(2,1)S(1)}, bf16[4,64,128]{2,1,0:T(8,128)(2,1)S(1)}, u32[]{:S(2)}, u32[]{:S(2)}) collective-permute-start(bf16[4,64,128]{2,1,0:T(8,128)(2,1)S(1)} %get-tuple-element.148), channel_id=1, source_target_pairs={{1,0},{0,1},{3,2},{2,3},{5,4},{4,5},{7,6},{6,7},{9,8},{8,9},{11,10... | collective-permute-start | bytes 196616 | tf_op jit(solution)/shard_map/ppermute | solution.py:26
  40.1 4.3 %collective-permute-start.10 = (bf16[4,64,128]{2,1,0:T(8,128)(2,1)S(1)}, bf16[4,64,128]{2,1,0:T(8,128)(2,1)S(1)}, u32[]{:S(2)}, u32[]{:S(2)}) collective-permute-start(bf16[4,64,128]{2,1,0:T(8,128)(2,1)S(1)} %get-tuple-element.147), channel_id=1, source_target_pairs={{0,1},{1,0},{2,3},{3,2},{4,5},{5,4},{6,7},{7,6},{8,9},{9,8},{10,11... | collective-permute-start | bytes 196616 | tf_op jit(solution)/shard_map/ppermute | solution.py:23
  45.9 4.3 %collective-permute-start.13 = (bf16[4,64,128]{2,1,0:T(8,128)(2,1)S(1)}, bf16[4,64,128]{2,1,0:T(8,128)(2,1)S(1)}, u32[]{:S(2)}, u32[]{:S(2)}) collective-permute-start(bf16[4,64,128]{2,1,0:T(8,128)(2,1)S(1)} %get-tuple-element.146), channel_id=1, source_target_pairs={{1,0},{0,1},{3,2},{2,3},{5,4},{4,5},{7,6},{6,7},{9,8},{8,9},{11,10... | collective-permute-start | bytes 196616 | tf_op jit(solution)/shard_map/ppermute | solution.py:26
  47.0 4.3 %collective-permute-start.12 = (bf16[4,64,128]{2,1,0:T(8,128)(2,1)S(1)}, bf16[4,64,128]{2,1,0:T(8,128)(2,1)S(1)}, u32[]{:S(2)}, u32[]{:S(2)}) collective-permute-start(bf16[4,64,128]{2,1,0:T(8,128)(2,1)S(1)} %get-tuple-element.145), channel_id=1, source_target_pairs={{0,1},{1,0},{2,3},{3,2},{4,5},{5,4},{6,7},{7,6},{8,9},{9,8},{10,11... | collective-permute-start | bytes 196616 | tf_op jit(solution)/shard_map/ppermute | solution.py:23
  52.6 2.1 copy-start.7
  52.6 21.2 %collective-permute-start.15 = (bf16[4,64,128]{2,1,0:T(8,128)(2,1)S(1)}, bf16[4,64,128]{2,1,0:T(8,128)(2,1)S(1)}, u32[]{:S(2)}, u32[]{:S(2)}) collective-permute-start(bf16[4,64,128]{2,1,0:T(8,128)(2,1)S(1)} %get-tuple-element.144), channel_id=1, source_target_pairs={{1,0},{0,1},{3,2},{2,3},{5,4},{4,5},{7,6},{6,7},{9,8},{8,9},{11,10... | collective-permute-start | bytes 196616 | tf_op jit(solution)/shard_map/ppermute | solution.py:26
  53.7 20.2 %collective-permute-start.14 = (bf16[4,64,128]{2,1,0:T(8,128)(2,1)S(1)}, bf16[4,64,128]{2,1,0:T(8,128)(2,1)S(1)}, u32[]{:S(2)}, u32[]{:S(2)}) collective-permute-start(bf16[4,64,128]{2,1,0:T(8,128)(2,1)S(1)} %get-tuple-element.143), channel_id=1, source_target_pairs={{0,1},{1,0},{2,3},{3,2},{4,5},{5,4},{6,7},{7,6},{8,9},{9,8},{10,11... | collective-permute-start | bytes 196616 | tf_op jit(solution)/shard_map/ppermute | solution.py:23
  112.0 6.3 %collective-permute-start.16 = (bf16[8,64,128]{2,1,0:T(8,128)(2,1)S(1)}, bf16[8,64,128]{2,1,0:T(8,128)(2,1)S(1)}, u32[]{:S(2)}, u32[]{:S(2)}) collective-permute-start(bf16[8,64,128]{2,1,0:T(8,128)(2,1)S(1)} %get-tuple-element.159), channel_id=1, source_target_pairs={{0,2},{2,4},{4,6},{6,8},{8,10},{10,12},{12,14},{14,16},{16,18},{18... | collective-permute-start | bytes 393224 | tf_op jit(solution)/shard_map/ppermute | solution.py:47
  118.4 4.3 %collective-permute-start.18 = (bf16[4,64,128]{2,1,0:T(8,128)(2,1)S(1)}, bf16[4,64,128]{2,1,0:T(8,128)(2,1)S(1)}, u32[]{:S(2)}, u32[]{:S(2)}) collective-permute-start(bf16[4,64,128]{2,1,0:T(8,128)(2,1)S(1)} %get-tuple-element.142), channel_id=1, source_target_pairs={{1,0},{0,1},{3,2},{2,3},{5,4},{4,5},{7,6},{6,7},{9,8},{8,9},{11,10... | collective-permute-start | bytes 196616 | tf_op jit(solution)/shard_map/ppermute | solution.py:26
  119.5 4.3 %collective-permute-start.17 = (bf16[4,64,128]{2,1,0:T(8,128)(2,1)S(1)}, bf16[4,64,128]{2,1,0:T(8,128)(2,1)S(1)}, u32[]{:S(2)}, u32[]{:S(2)}) collective-permute-start(bf16[4,64,128]{2,1,0:T(8,128)(2,1)S(1)} %get-tuple-element.141), channel_id=1, source_target_pairs={{0,1},{1,0},{2,3},{3,2},{4,5},{5,4},{6,7},{7,6},{8,9},{9,8},{10,11... | collective-permute-start | bytes 196616 | tf_op jit(solution)/shard_map/ppermute | solution.py:23
  125.1 4.3 %collective-permute-start.20 = (bf16[4,64,128]{2,1,0:T(8,128)(2,1)S(1)}, bf16[4,64,128]{2,1,0:T(8,128)(2,1)S(1)}, u32[]{:S(2)}, u32[]{:S(2)}) collective-permute-start(bf16[4,64,128]{2,1,0:T(8,128)(2,1)S(1)} %get-tuple-element.140), channel_id=1, source_target_pairs={{1,0},{0,1},{3,2},{2,3},{5,4},{4,5},{7,6},{6,7},{9,8},{8,9},{11,10... | collective-permute-start | bytes 196616 | tf_op jit(solution)/shard_map/ppermute | solution.py:26
  126.2 4.6 %collective-permute-start.19 = (bf16[4,64,128]{2,1,0:T(8,128)(2,1)S(1)}, bf16[4,64,128]{2,1,0:T(8,128)(2,1)S(1)}, u32[]{:S(2)}, u32[]{:S(2)}) collective-permute-start(bf16[4,64,128]{2,1,0:T(8,128)(2,1)S(1)} %get-tuple-element.139), channel_id=1, source_target_pairs={{0,1},{1,0},{2,3},{3,2},{4,5},{5,4},{6,7},{7,6},{8,9},{9,8},{10,11... | collective-permute-start | bytes 196616 | tf_op jit(solution)/shard_map/ppermute | solution.py:23
  132.4 5.0 %collective-permute-start.22 = (bf16[4,64,128]{2,1,0:T(8,128)(2,1)S(1)}, bf16[4,64,128]{2,1,0:T(8,128)(2,1)S(1)}, u32[]{:S(2)}, u32[]{:S(2)}) collective-permute-start(bf16[4,64,128]{2,1,0:T(8,128)(2,1)S(1)} %get-tuple-element.138), channel_id=1, source_target_pairs={{1,0},{0,1},{3,2},{2,3},{5,4},{4,5},{7,6},{6,7},{9,8},{8,9},{11,10... | collective-permute-start | bytes 196616 | tf_op jit(solution)/shard_map/ppermute | solution.py:26
  133.4 5.1 %collective-permute-start.21 = (bf16[4,64,128]{2,1,0:T(8,128)(2,1)S(1)}, bf16[4,64,128]{2,1,0:T(8,128)(2,1)S(1)}, u32[]{:S(2)}, u32[]{:S(2)}) collective-permute-start(bf16[4,64,128]{2,1,0:T(8,128)(2,1)S(1)} %get-tuple-element.137), channel_id=1, source_target_pairs={{0,1},{1,0},{2,3},{3,2},{4,5},{5,4},{6,7},{7,6},{8,9},{9,8},{10,11... | collective-permute-start | bytes 196616 | tf_op jit(solution)/shard_map/ppermute | solution.py:23
  139.9 4.8 %collective-permute-start.24 = (bf16[4,64,128]{2,1,0:T(8,128)(2,1)S(1)}, bf16[4,64,128]{2,1,0:T(8,128)(2,1)S(1)}, u32[]{:S(2)}, u32[]{:S(2)}) collective-permute-start(bf16[4,64,128]{2,1,0:T(8,128)(2,1)S(1)} %get-tuple-element.136), channel_id=1, source_target_pairs={{1,0},{0,1},{3,2},{2,3},{5,4},{4,5},{7,6},{6,7},{9,8},{8,9},{11,10... | collective-permute-start | bytes 196616 | tf_op jit(solution)/shard_map/ppermute | solution.py:26
  141.0 4.5 %collective-permute-start.23 = (bf16[4,64,128]{2,1,0:T(8,128)(2,1)S(1)}, bf16[4,64,128]{2,1,0:T(8,128)(2,1)S(1)}, u32[]{:S(2)}, u32[]{:S(2)}) collective-permute-start(bf16[4,64,128]{2,1,0:T(8,128)(2,1)S(1)} %get-tuple-element.135), channel_id=1, source_target_pairs={{0,1},{1,0},{2,3},{3,2},{4,5},{5,4},{6,7},{7,6},{8,9},{9,8},{10,11... | collective-permute-start | bytes 196616 | tf_op jit(solution)/shard_map/ppermute | solution.py:23
  147.0 4.3 %collective-permute-start.26 = (bf16[4,64,128]{2,1,0:T(8,128)(2,1)S(1)}, bf16[4,64,128]{2,1,0:T(8,128)(2,1)S(1)}, u32[]{:S(2)}, u32[]{:S(2)}) collective-permute-start(bf16[4,64,128]{2,1,0:T(8,128)(2,1)S(1)} %get-tuple-element.134), channel_id=1, source_target_pairs={{1,0},{0,1},{3,2},{2,3},{5,4},{4,5},{7,6},{6,7},{9,8},{8,9},{11,10... | collective-permute-start | bytes 196616 | tf_op jit(solution)/shard_map/ppermute | solution.py:26
  148.1 4.3 %collective-permute-start.25 = (bf16[4,64,128]{2,1,0:T(8,128)(2,1)S(1)}, bf16[4,64,128]{2,1,0:T(8,128)(2,1)S(1)}, u32[]{:S(2)}, u32[]{:S(2)}) collective-permute-start(bf16[4,64,128]{2,1,0:T(8,128)(2,1)S(1)} %get-tuple-element.133), channel_id=1, source_target_pairs={{0,1},{1,0},{2,3},{3,2},{4,5},{5,4},{6,7},{7,6},{8,9},{9,8},{10,11... | collective-permute-start | bytes 196616 | tf_op jit(solution)/shard_map/ppermute | solution.py:23
  153.7 4.3 %collective-permute-start.28 = (bf16[4,64,128]{2,1,0:T(8,128)(2,1)S(1)}, bf16[4,64,128]{2,1,0:T(8,128)(2,1)S(1)}, u32[]{:S(2)}, u32[]{:S(2)}) collective-permute-start(bf16[4,64,128]{2,1,0:T(8,128)(2,1)S(1)} %get-tuple-element.132), channel_id=1, source_target_pairs={{1,0},{0,1},{3,2},{2,3},{5,4},{4,5},{7,6},{6,7},{9,8},{8,9},{11,10... | collective-permute-start | bytes 196616 | tf_op jit(solution)/shard_map/ppermute | solution.py:26
  154.8 4.3 %collective-permute-start.27 = (bf16[4,64,128]{2,1,0:T(8,128)(2,1)S(1)}, bf16[4,64,128]{2,1,0:T(8,128)(2,1)S(1)}, u32[]{:S(2)}, u32[]{:S(2)}) collective-permute-start(bf16[4,64,128]{2,1,0:T(8,128)(2,1)S(1)} %get-tuple-element.131), channel_id=1, source_target_pairs={{0,1},{1,0},{2,3},{3,2},{4,5},{5,4},{6,7},{7,6},{8,9},{9,8},{10,11... | collective-permute-start | bytes 196616 | tf_op jit(solution)/shard_map/ppermute | solution.py:23
  160.6 4.3 %collective-permute-start.30 = (bf16[4,64,128]{2,1,0:T(8,128)(2,1)S(1)}, bf16[4,64,128]{2,1,0:T(8,128)(2,1)S(1)}, u32[]{:S(2)}, u32[]{:S(2)}) collective-permute-start(bf16[4,64,128]{2,1,0:T(8,128)(2,1)S(1)} %get-tuple-element.130), channel_id=1, source_target_pairs={{1,0},{0,1},{3,2},{2,3},{5,4},{4,5},{7,6},{6,7},{9,8},{8,9},{11,10... | collective-permute-start | bytes 196616 | tf_op jit(solution)/shard_map/ppermute | solution.py:26
  161.7 4.3 %collective-permute-start.29 = (bf16[4,64,128]{2,1,0:T(8,128)(2,1)S(1)}, bf16[4,64,128]{2,1,0:T(8,128)(2,1)S(1)}, u32[]{:S(2)}, u32[]{:S(2)}) collective-permute-start(bf16[4,64,128]{2,1,0:T(8,128)(2,1)S(1)} %get-tuple-element.129), channel_id=1, source_target_pairs={{0,1},{1,0},{2,3},{3,2},{4,5},{5,4},{6,7},{7,6},{8,9},{9,8},{10,11... | collective-permute-start | bytes 196616 | tf_op jit(solution)/shard_map/ppermute | solution.py:23
  167.3 4.3 %collective-permute-start.32 = (bf16[4,64,128]{2,1,0:T(8,128)(2,1)S(1)}, bf16[4,64,128]{2,1,0:T(8,128)(2,1)S(1)}, u32[]{:S(2)}, u32[]{:S(2)}) collective-permute-start(bf16[4,64,128]{2,1,0:T(8,128)(2,1)S(1)} %get-tuple-element.128), channel_id=1, source_target_pairs={{1,0},{0,1},{3,2},{2,3},{5,4},{4,5},{7,6},{6,7},{9,8},{8,9},{11,10... | collective-permute-start | bytes 196616 | tf_op jit(solution)/shard_map/ppermute | solution.py:26
  168.4 4.3 %collective-permute-start.31 = (bf16[4,64,128]{2,1,0:T(8,128)(2,1)S(1)}, bf16[4,64,128]{2,1,0:T(8,128)(2,1)S(1)}, u32[]{:S(2)}, u32[]{:S(2)}) collective-permute-start(bf16[4,64,128]{2,1,0:T(8,128)(2,1)S(1)} %get-tuple-element.127), channel_id=1, source_target_pairs={{0,1},{1,0},{2,3},{3,2},{4,5},{5,4},{6,7},{7,6},{8,9},{9,8},{10,11... | collective-permute-start | bytes 196616 | tf_op jit(solution)/shard_map/ppermute | solution.py:23
  173.4 1.0 copy-start.4
  174.8 18.0 %copy-start.5 = (f32[8,64,128]{2,1,0:T(8,128)}, f32[8,64,128]{2,1,0:T(8,128)S(1)}, u32[]{:S(2)}) copy-start(f32[8,64,128]{2,1,0:T(8,128)S(1)} %fusion.11) | copy-start | bytes 786436
  208.0 6.3 %collective-permute-start.33 = (bf16[8,64,128]{2,1,0:T(8,128)(2,1)S(1)}, bf16[8,64,128]{2,1,0:T(8,128)(2,1)S(1)}, u32[]{:S(2)}, u32[]{:S(2)}) collective-permute-start(bf16[8,64,128]{2,1,0:T(8,128)(2,1)S(1)} %get-tuple-element.161), channel_id=1, source_target_pairs={{0,2},{2,4},{4,6},{6,8},{8,10},{10,12},{12,14},{14,16},{16,18},{18... | collective-permute-start | bytes 393224 | tf_op jit(solution)/shard_map/ppermute | solution.py:47
  214.4 4.3 %collective-permute-start.35 = (bf16[4,64,128]{2,1,0:T(8,128)(2,1)S(1)}, bf16[4,64,128]{2,1,0:T(8,128)(2,1)S(1)}, u32[]{:S(2)}, u32[]{:S(2)}) collective-permute-start(bf16[4,64,128]{2,1,0:T(8,128)(2,1)S(1)} %get-tuple-element.126), channel_id=1, source_target_pairs={{1,0},{0,1},{3,2},{2,3},{5,4},{4,5},{7,6},{6,7},{9,8},{8,9},{11,10... | collective-permute-start | bytes 196616 | tf_op jit(solution)/shard_map/ppermute | solution.py:26
  215.5 4.3 %collective-permute-start.34 = (bf16[4,64,128]{2,1,0:T(8,128)(2,1)S(1)}, bf16[4,64,128]{2,1,0:T(8,128)(2,1)S(1)}, u32[]{:S(2)}, u32[]{:S(2)}) collective-permute-start(bf16[4,64,128]{2,1,0:T(8,128)(2,1)S(1)} %get-tuple-element.125), channel_id=1, source_target_pairs={{0,1},{1,0},{2,3},{3,2},{4,5},{5,4},{6,7},{7,6},{8,9},{9,8},{10,11... | collective-permute-start | bytes 196616 | tf_op jit(solution)/shard_map/ppermute | solution.py:23
  221.2 4.3 %collective-permute-start.37 = (bf16[4,64,128]{2,1,0:T(8,128)(2,1)S(1)}, bf16[4,64,128]{2,1,0:T(8,128)(2,1)S(1)}, u32[]{:S(2)}, u32[]{:S(2)}) collective-permute-start(bf16[4,64,128]{2,1,0:T(8,128)(2,1)S(1)} %get-tuple-element.124), channel_id=1, source_target_pairs={{1,0},{0,1},{3,2},{2,3},{5,4},{4,5},{7,6},{6,7},{9,8},{8,9},{11,10... | collective-permute-start | bytes 196616 | tf_op jit(solution)/shard_map/ppermute | solution.py:26
  222.2 4.8 %collective-permute-start.36 = (bf16[4,64,128]{2,1,0:T(8,128)(2,1)S(1)}, bf16[4,64,128]{2,1,0:T(8,128)(2,1)S(1)}, u32[]{:S(2)}, u32[]{:S(2)}) collective-permute-start(bf16[4,64,128]{2,1,0:T(8,128)(2,1)S(1)} %get-tuple-element.123), channel_id=1, source_target_pairs={{0,1},{1,0},{2,3},{3,2},{4,5},{5,4},{6,7},{7,6},{8,9},{9,8},{10,11... | collective-permute-start | bytes 196616 | tf_op jit(solution)/shard_map/ppermute | solution.py:23
  228.6 5.0 %collective-permute-start.39 = (bf16[4,64,128]{2,1,0:T(8,128)(2,1)S(1)}, bf16[4,64,128]{2,1,0:T(8,128)(2,1)S(1)}, u32[]{:S(2)}, u32[]{:S(2)}) collective-permute-start(bf16[4,64,128]{2,1,0:T(8,128)(2,1)S(1)} %get-tuple-element.122), channel_id=1, source_target_pairs={{1,0},{0,1},{3,2},{2,3},{5,4},{4,5},{7,6},{6,7},{9,8},{8,9},{11,10... | collective-permute-start | bytes 196616 | tf_op jit(solution)/shard_map/ppermute | solution.py:26
  229.7 4.9 %collective-permute-start.38 = (bf16[4,64,128]{2,1,0:T(8,128)(2,1)S(1)}, bf16[4,64,128]{2,1,0:T(8,128)(2,1)S(1)}, u32[]{:S(2)}, u32[]{:S(2)}) collective-permute-start(bf16[4,64,128]{2,1,0:T(8,128)(2,1)S(1)} %get-tuple-element.121), channel_id=1, source_target_pairs={{0,1},{1,0},{2,3},{3,2},{4,5},{5,4},{6,7},{7,6},{8,9},{9,8},{10,11... | collective-permute-start | bytes 196616 | tf_op jit(solution)/shard_map/ppermute | solution.py:23
  235.9 4.7 %collective-permute-start.41 = (bf16[4,64,128]{2,1,0:T(8,128)(2,1)S(1)}, bf16[4,64,128]{2,1,0:T(8,128)(2,1)S(1)}, u32[]{:S(2)}, u32[]{:S(2)}) collective-permute-start(bf16[4,64,128]{2,1,0:T(8,128)(2,1)S(1)} %get-tuple-element.120), channel_id=1, source_target_pairs={{1,0},{0,1},{3,2},{2,3},{5,4},{4,5},{7,6},{6,7},{9,8},{8,9},{11,10... | collective-permute-start | bytes 196616 | tf_op jit(solution)/shard_map/ppermute | solution.py:26
  237.0 4.3 %collective-permute-start.40 = (bf16[4,64,128]{2,1,0:T(8,128)(2,1)S(1)}, bf16[4,64,128]{2,1,0:T(8,128)(2,1)S(1)}, u32[]{:S(2)}, u32[]{:S(2)}) collective-permute-start(bf16[4,64,128]{2,1,0:T(8,128)(2,1)S(1)} %get-tuple-element.119), channel_id=1, source_target_pairs={{0,1},{1,0},{2,3},{3,2},{4,5},{5,4},{6,7},{7,6},{8,9},{9,8},{10,11... | collective-permute-start | bytes 196616 | tf_op jit(solution)/shard_map/ppermute | solution.py:23
  242.8 4.3 %collective-permute-start.43 = (bf16[4,64,128]{2,1,0:T(8,128)(2,1)S(1)}, bf16[4,64,128]{2,1,0:T(8,128)(2,1)S(1)}, u32[]{:S(2)}, u32[]{:S(2)}) collective-permute-start(bf16[4,64,128]{2,1,0:T(8,128)(2,1)S(1)} %get-tuple-element.118), channel_id=1, source_target_pairs={{1,0},{0,1},{3,2},{2,3},{5,4},{4,5},{7,6},{6,7},{9,8},{8,9},{11,10... | collective-permute-start | bytes 196616 | tf_op jit(solution)/shard_map/ppermute | solution.py:26
  243.9 4.3 %collective-permute-start.42 = (bf16[4,64,128]{2,1,0:T(8,128)(2,1)S(1)}, bf16[4,64,128]{2,1,0:T(8,128)(2,1)S(1)}, u32[]{:S(2)}, u32[]{:S(2)}) collective-permute-start(bf16[4,64,128]{2,1,0:T(8,128)(2,1)S(1)} %get-tuple-element.117), channel_id=1, source_target_pairs={{0,1},{1,0},{2,3},{3,2},{4,5},{5,4},{6,7},{7,6},{8,9},{9,8},{10,11... | collective-permute-start | bytes 196616 | tf_op jit(solution)/shard_map/ppermute | solution.py:23
  249.5 4.3 %collective-permute-start.45 = (bf16[4,64,128]{2,1,0:T(8,128)(2,1)S(1)}, bf16[4,64,128]{2,1,0:T(8,128)(2,1)S(1)}, u32[]{:S(2)}, u32[]{:S(2)}) collective-permute-start(bf16[4,64,128]{2,1,0:T(8,128)(2,1)S(1)} %get-tuple-element.116), channel_id=1, source_target_pairs={{1,0},{0,1},{3,2},{2,3},{5,4},{4,5},{7,6},{6,7},{9,8},{8,9},{11,10... | collective-permute-start | bytes 196616 | tf_op jit(solution)/shard_map/ppermute | solution.py:26
  250.6 4.3 %collective-permute-start.44 = (bf16[4,64,128]{2,1,0:T(8,128)(2,1)S(1)}, bf16[4,64,128]{2,1,0:T(8,128)(2,1)S(1)}, u32[]{:S(2)}, u32[]{:S(2)}) collective-permute-start(bf16[4,64,128]{2,1,0:T(8,128)(2,1)S(1)} %get-tuple-element.115), channel_id=1, source_target_pairs={{0,1},{1,0},{2,3},{3,2},{4,5},{5,4},{6,7},{7,6},{8,9},{9,8},{10,11... | collective-permute-start | bytes 196616 | tf_op jit(solution)/shard_map/ppermute | solution.py:23
  255.8 1.0 copy-start.6
where the time goes:
time: 260 us; the launch traced here: 258 us
  waiting for transfers between devices  77.3 us (30%)
  blocking collectives  58.2 us (22%)
  starting transfers between devices  52.7 us (20%)
  matrix products  42.4 us (16%)
  local copies, waits for them, and re-layouts  19.6 us (8%)
  other arithmetic  4.94 us (2%)
    all_gather x3, blocking collectives, carried_in(): gathered = jax.tree.map(lambda a: lax.all_gather(a, axis), part)  58.2 us
    ppermute x22, waiting for transfers between devices, extended(): lax.ppermute(lax.slice_in_dim(block, 0, width, axis=dim), axis, backward)  49.6 us
    dot_general x28, matrix products, compose(): jnp.einsum('bpq,bqe->bpe', later[0], earlier[1], precision=highest)  26.6 us
    ppermute x22, starting transfers between devices, extended(): lax.ppermute(lax.slice_in_dim(block, 0, width, axis=dim), axis, backward)  24.2 us
    ppermute x22, waiting for transfers between devices, extended(): lax.ppermute(lax.slice_in_dim(block, block.shape[dim] - width, None, axis...  21.9 us
    ppermute x22, starting transfers between devices, extended(): lax.ppermute(lax.slice_in_dim(block, block.shape[dim] - width, None, axis...  21.8 us
    gather x22, local copies, waits for them, and re-layouts, coupling(): picked = jnp.take(source, positions, axis=0)  15.4 us
    dot_general x33, matrix products, apply_inverse(): jnp.einsum('bij,bje->bie', diag_blocks, values.astype(jnp.bfloat16), pref...  12.7 us
  transfers between devices with their start and end apart: 46, of which 44 were waited for; matrix products, arithmetic and copies ran while one was open for 0% of the time, Pallas kernels for 0%

commit v1 on v0

--- a/solution.py
+++ b/solution.py
@@ -1,6 +1,10 @@
+import functools
+
 import jax
 import jax.numpy as jnp
 from jax import lax
+from jax.experimental import pallas as pl
+from jax.experimental.pallas import tpu as pltpu
 from jax.sharding import PartitionSpec as P
 
 BRICK = 64
@@ -9,9 +13,13 @@
 SWEEPS = 3
 STEPS = 4
 ITERS = 2
-
+GROUP = REACH
 
 highest = lax.Precision.HIGHEST
+f32 = jnp.float32
+bf16 = jnp.bfloat16
+VMEM = pl.BlockSpec(memory_space=pltpu.VMEM)
+SMEM = pl.BlockSpec(memory_space=pltpu.SMEM)
 
 
 def extended(block, sides, width):
@@ -67,7 +75,7 @@
     return jnp.mod(indices - position[:, None] + REACH, bricks_all) - REACH
 
 
-def body(initial, forcing, brick_blocks, neighbours, coarse_modes, coarse_blocks):
+def banded_body(initial, forcing, brick_blocks, neighbours, coarse_modes, coarse_blocks):
     bricks_here = initial.shape[0]
     bricks_all = bricks_here * lax.axis_size("space")
     first_brick = lax.axis_index("space") * bricks_here
@@ -121,6 +129,279 @@
     return (jnp.stack(outputs, 0), defect[None])
 
 
+def dot(a, b):
+    return jnp.dot(a, b, preferred_element_type=f32)
+
+
+def dot_f32(a, b):
+    return jnp.dot(a, b, preferred_element_type=f32, precision=highest)
+
+
+def operator_kernel(parts, bits, info, nbr, *refs):
+    blocks = refs[:parts]
+    modes_t, modes, coarse, phi, images, powers, shifts, off, diag, lin = refs[parts:]
+    here = blocks[0].shape[0]
+    bricks = here * parts
+    rows = bricks * BRICK
+    groups = bricks // GROUP
+    span = GROUP * BRICK
+    wide = rows // 128
+    lane = lax.broadcasted_iota(jnp.int32, (BRICK, 128), 1)
+    left = lane < BRICK
+    off[...] = jnp.zeros_like(off)
+    diag[...] = jnp.zeros_like(diag)
+    for b in range(bricks):
+        source = blocks[b // here]
+        r = b % here
+        slots = source.shape[2] // BRICK
+        for s in range(slots):
+            tile = source[r, :, pl.ds((s // 2) * 128, min(128, source.shape[2] - (s // 2) * 128))]
+            tile = tile.astype(f32)[:, (s % 2) * BRICK:(s % 2 + 1) * BRICK]
+            both = jnp.concatenate([tile, tile], axis=1)
+            if s == 0:
+                keep = left if b % 2 == 0 else jnp.logical_not(left)
+                at = (b % GROUP) // 2
+                diag[pl.ds(b * BRICK, BRICK), pl.ds(at * 128, 128)] = jnp.where(
+                    keep, both, 0.0
+                ).astype(bf16)
+            else:
+                place = nbr[b, s - 1]
+                half = lax.rem(place, 2)
+                keep = (lane // BRICK) == half
+                at = lax.div(place, 2)
+                old = off[at, pl.ds(b * BRICK, BRICK), :]
+                off[at, pl.ds(b * BRICK, BRICK), :] = old + jnp.where(keep, both, 0.0).astype(bf16)
+
+    def near(r, k):
+        return (r - k) % groups in (0, 1, groups - 1)
+
+    for k in range(groups):
+        d = diag[pl.ds(k * span, span), :]
+        for r in range(groups):
+            if near(r, k):
+                o = jnp.concatenate(
+                    [off[k * (span // 128) + i, pl.ds(r * span, span), :] for i in range(span // 128)],
+                    axis=1,
+                )
+                lin[pl.ds(r * span, span), pl.ds(k * span, span)] = dot(o, d).astype(bf16)
+    for n in range(groups):
+        for r in range(groups):
+            acc = None
+            for k in range(groups):
+                if near(r, k) and near(k, n):
+                    part = dot(
+                        lin[pl.ds(r * span, span), pl.ds(k * span, span)],
+                        lin[pl.ds(k * span, span), pl.ds(n * span, span)],
+                    )
+                    acc = part if acc is None else acc + part
+            d = diag[pl.ds(r * span, span), :]
+            body = -acc if acc is not None else None
+            if near(r, n):
+                first = lin[pl.ds(r * span, span), pl.ds(n * span, span)].astype(f32)
+                body = first if body is None else first + body
+            out = jnp.zeros((span, span), f32) if body is None else -dot(d, body.astype(bf16))
+            if r == n:
+                out = out + d.astype(f32)
+            phi[pl.ds(r * span, span), pl.ds(n * span, span)] = out.astype(bf16)
+    own = here * BRICK
+    image = modes_t[...]
+    for i in range(STEPS):
+        full = dot(phi[...], image)
+        image = full.astype(bf16)
+        images[i] = image[:own]
+    size = bricks * Q
+    a = coarse[...]
+    m = modes[...]
+    k = dot_f32(m, full)
+    gram = lax.dot_general(m, m, (((1,), (1,)), ((), ())), preferred_element_type=f32, precision=highest)
+    lower = k - dot_f32(gram, a)
+    step = jnp.concatenate(
+        [
+            jnp.concatenate([a, jnp.zeros((size, size), f32)], axis=1),
+            jnp.concatenate([lower, a], axis=1),
+        ],
+        axis=0,
+    )
+    row = lax.broadcasted_iota(jnp.int32, (2 * size, 2 * size), 0)
+    col = lax.broadcasted_iota(jnp.int32, (2 * size, 2 * size), 1)
+    moved = (row == col).astype(f32)
+    for i in range(bits):
+        powers[i] = step
+        bit = info[i]
+        shifts[i] = moved * (bit == 1).astype(f32)
+        if i < bits - 1:
+            moved = jnp.where(bit == 1, dot_f32(moved, step), moved)
+            step = dot_f32(step, step)
+
+
+def chain_kernel(parts, phi, first, force, modes, far_term, *refs):
+    far_first = refs[:parts - 1]
+    far_force = refs[parts - 1:2 * parts - 2]
+    iterates, start = refs[2 * parts - 2:]
+    own = first.shape[0]
+    current = jnp.concatenate([first[...]] + [r[...] for r in far_first], axis=0)
+    for i in range(STEPS - 1):
+        full = dot(phi[...], current)
+        mine = full[:own] + force[i].astype(f32)
+        iterates[i] = mine
+        current = jnp.concatenate(
+            [mine.astype(bf16)]
+            + [
+                (full[own * (p + 1):own * (p + 2)] + far_force[p][i].astype(f32)).astype(bf16)
+                for p in range(parts - 1)
+            ],
+            axis=0,
+        )
+    full = dot(phi[...], current)
+    mine = full[:own] + force[STEPS - 1].astype(f32)
+    iterates[STEPS - 1] = mine
+    g = dot_f32(modes[...], jnp.concatenate([mine, full[own:]], axis=0)) + far_term[...]
+    size = g.shape[0]
+    m = modes[...]
+    gram = lax.dot_general(m, m, (((1,), (1,)), ((), ())), preferred_element_type=f32, precision=highest)
+    start[pl.ds(0, size), :] = g
+    start[pl.ds(size, size), :] = g - dot_f32(gram, g)
+
+
+def join_kernel(bit, power, shift, mine, other, before, total, prefix):
+    upper = bit[0] == 1
+    low = jnp.where(upper, other[...], mine[...])
+    high = jnp.where(upper, mine[...], other[...])
+    total[...] = dot_f32(power[...], low) + high
+    prefix[...] = before[...] + dot_f32(shift[...], low)
+
+
+def last_kernel(shift, other, before, step, start, images, modes_t, iterates, solution, defect):
+    prefix = before[...] + dot_f32(shift[...], other[...])
+    size = prefix.shape[0] // 2
+    here = defect.shape[0]
+    mine = dot_f32(step[...], prefix) + start[...]
+    first = mine[:size]
+    both = first + mine[size:]
+    m = modes_t[...]
+    shape = defect.shape
+    came = (prefix[:size] + prefix[size:]).astype(bf16)
+    for i in range(STEPS - 1):
+        solution[i] = (iterates[i] + dot(images[i], came)).reshape(shape)
+    solution[STEPS - 1] = dot_f32(m, both).reshape(shape)
+    defect[...] = (
+        iterates[STEPS - 1] + dot(images[STEPS - 1], prefix[:size].astype(bf16)) - dot_f32(m, first)
+    ).reshape(shape)
+
+
+def dense_body(initial, forcing, brick_blocks, neighbours, coarse_modes, coarse_blocks):
+    here = initial.shape[0]
+    ens = initial.shape[2]
+    parts = lax.axis_size("space")
+    bricks = here * parts
+    own = here * BRICK
+    rows = bricks * BRICK
+    slices = lax.axis_size("tm")
+    bits = slices.bit_length() - 1
+    first_brick = lax.axis_index("space") * here
+    place = lax.axis_index("tm")
+
+    def others(value):
+        return [
+            lax.ppermute(value, "space", [((s + k) % parts, s) for s in range(parts)])
+            for k in range(1, parts)
+        ]
+
+    far_blocks = others(brick_blocks)
+    force = forcing.reshape(STEPS, own, ens)
+    last_term = jnp.einsum(
+        "qc,bce->bqe", coarse_modes, forcing[STEPS - 1].astype(f32), precision=highest
+    ).reshape(here * Q, ens)
+    small = jnp.concatenate(
+        [
+            last_term,
+            jnp.pad(coarse_blocks.reshape(here * Q, Q), ((0, 0), (0, ens - Q))),
+            jnp.pad(neighbours.astype(f32), ((0, 0), (0, ens - neighbours.shape[1]))),
+        ],
+        axis=0,
+    )
+    far_small = others(small)
+    far_force = others(force[:STEPS - 1])
+    start_half = initial.astype(bf16).reshape(own, ens)
+    far_first = [
+        lax.ppermute(
+            start_half, ("tm", "space"), [((s + k) % parts, s) for s in range(parts)]
+        )
+        for k in range(1, parts)
+    ]
+    first = jnp.where(place == 0, start_half, jnp.zeros_like(start_half))
+
+    slots = neighbours.shape[1]
+    nbr = jnp.concatenate(
+        [neighbours] + [f[2 * here * Q:, :slots].astype(jnp.int32) for f in far_small], axis=0
+    )
+    nbr = jnp.mod(nbr - first_brick, bricks)
+    coarse_all = jnp.concatenate(
+        [coarse_blocks.reshape(here * Q, Q)] + [f[here * Q:2 * here * Q, :Q] for f in far_small],
+        axis=0,
+    )
+    far_term = jnp.concatenate(
+        [jnp.zeros_like(last_term)] + [f[:here * Q] for f in far_small], axis=0
+    )
+    size = bricks * Q
+    grid_row = lax.broadcasted_iota(jnp.int32, (size, size), 0) // Q
+    grid_col = lax.broadcasted_iota(jnp.int32, (size, size), 1) // Q
+    coarse = jnp.where(grid_row == grid_col, jnp.tile(coarse_all, (1, bricks)), 0.0)
+    mode_row = lax.broadcasted_iota(jnp.int32, (size, rows), 0) // Q
+    mode_col = lax.broadcasted_iota(jnp.int32, (size, rows), 1) // BRICK
+    modes = jnp.where(mode_row == mode_col, jnp.tile(coarse_modes, (bricks, bricks)), 0.0)
+    modes_t = modes.T
+    info = jnp.stack([(place >> i) & 1 for i in range(bits)]).astype(jnp.int32)
+
+    sds = jax.ShapeDtypeStruct
+    phi, images, powers, shifts = pl.pallas_call(
+        functools.partial(operator_kernel, parts, bits),
+        out_shape=(
+            sds((rows, rows), bf16),
+            sds((STEPS, own, size), bf16),
+            sds((bits, 2 * size, 2 * size), f32),
+            sds((bits, 2 * size, 2 * size), f32),
+        ),
+        in_specs=[SMEM, SMEM] + [VMEM] * (parts + 3),
+        out_specs=(VMEM,) * 4,
+        scratch_shapes=[
+            pltpu.VMEM((rows // 128, rows, 128), bf16),
+            pltpu.VMEM((rows, GROUP * BRICK), bf16),
+            pltpu.VMEM((rows, rows), bf16),
+        ],
+        name="operator",
+    )(info, nbr, brick_blocks, *far_blocks, modes_t.astype(bf16), modes, coarse)
+
+    iterates, start = pl.pallas_call(
+        functools.partial(chain_kernel, parts),
+        out_shape=(sds((STEPS, own, ens), f32), sds((2 * size, ens), f32)),
+        in_specs=[VMEM] * (5 + 2 * (parts - 1)),
+        out_specs=(VMEM,) * 2,
+        name="chain",
+    )(phi, first, force, modes, far_term, *far_first, *far_force)
+
+    total = start
+    prefix = jnp.zeros_like(start)
+    for i in range(bits):
+        other = lax.ppermute(total, "tm", [(j, j ^ (1 << i)) for j in range(slices)])
+        if i < bits - 1:
+            total, prefix = pl.pallas_call(
+                join_kernel,
+                out_shape=(sds((2 * size, ens), f32),) * 2,
+                in_specs=[SMEM] + [VMEM] * 5,
+                out_specs=(VMEM,) * 2,
+                name="join",
+            )(info[i:i + 1], powers[i], shifts[i], total, other, prefix)
+    solution_out, defect = pl.pallas_call(
+        last_kernel,
+        out_shape=(sds((STEPS, here, BRICK, ens), f32), sds((here, BRICK, ens), f32)),
+        in_specs=[VMEM] * 8,
+        out_specs=(VMEM,) * 2,
+        name="last",
+    )(shifts[bits - 1], other, prefix, powers[0], start, images, modes_t[:own], iterates)
+    return solution_out, defect[None]
+
+
 def solution(mesh):
     placed = (
         P("space", None, None),
@@ -130,6 +411,14 @@
         P(),
         P("space", None, None),
     )
+
+    def body(initial, *rest):
+        bricks = initial.shape[0] * lax.axis_size("space")
+        slices = lax.axis_size("tm")
+        fits = 8 * (bricks * BRICK) ** 2 <= 16 * 2 ** 20
+        even = bricks % GROUP == 0 and slices > 1 and slices & (slices - 1) == 0
+        return (dense_body if fits and even else banded_body)(initial, *rest)
+
     return jax.shard_map(
         body,
         mesh=mesh,

time: 260 us -> 84.7 us (0.33)
  the two profiles are of different devices: /device:TPU:26 before, /device:TPU:0 now
where the time goes in v1:
time: 84.7 us; the launch traced here: 84.1 us
  Pallas kernels  36.4 us (43%)
  waiting for transfers between devices  13.5 us (16%)
  local copies, waits for them, and re-layouts  13 us (15%)
  starting transfers between devices  12.7 us (15%)
  other arithmetic  6.63 us (8%)
  matrix products  1.07 us (1%)
    pallas_call x1, Pallas kernels, dense_body(): pl.pallas_call(functools.partial(operator_kernel, parts, bits), out_shape...  16.9 us
    ppermute x4, waiting for transfers between devices, dense_body(): other = lax.ppermute(total, 'tm', [(j, j ^ 1 << i) for j in range(slices)])  12.7 us
    pallas_call x1, Pallas kernels, dense_body(): pl.pallas_call(functools.partial(chain_kernel, parts), out_shape=(sds((ST...  7.8 us
    pallas_call x3, Pallas kernels, dense_body(): pl.pallas_call(join_kernel, out_shape=(sds((2 * size, ens), f32),) * 2, i...  7.39 us
    ppermute x4, starting transfers between devices, dense_body(): other = lax.ppermute(total, 'tm', [(j, j ^ 1 << i) for j in range(slices)])  5.69 us
    pallas_call x1, Pallas kernels, dense_body(): pl.pallas_call(last_kernel, out_shape=(sds((STEPS, here, BRICK, ens), f32...  4.38 us
    ppermute x1, starting transfers between devices, dense_body(): lax.ppermute(start_half, ('tm', 'space'), [((s + k) % parts, s) for s in...  3.85 us
    unnamed x18, local copies, waits for them, and re-layouts  3.58 us
  transfers between devices with their start and end apart: 8, of which 5 were waited for; matrix products, arithmetic and copies ran while one was open for 17% of the time, Pallas kernels for 20%

profile of v1, /device:TPU:0, one launch (start us, length us, event | category | flops | bytes accessed | tf_op | source)
XLA Modules:
  0.0 84.1 jit_solution(11665641120855295722)
XLA Ops:
  0.6 0.7 convert_element_type.17
  1.3 1.1 %convolution_bitcast_fusion = f32[64,128]{1,0:T(8,128)S(1)} fusion(bf16[4,8,64,128]{3,2,1,0:T(8,128)(2,1)} %param.7, f32[8,64]{1,0:T(8,128)} %param.10), kind=kOutput, calls=%fused_computation | convolution fusion | flops 6291456 | bytes 167936 | tf_op jit(solution)/shard_map/qc,bce->bqe/dot_general | solution.py:312
  2.4 0.8 select_maximum_fusion
  3.2 3.0 %collective-permute-start = (f32[136,128]{1,0:T(8,128)S(1)}, f32[136,128]{1,0:T(8,128)S(1)}, u32[]{:S(2)}, u32[]{:S(2)}) collective-permute-start(f32[136,128]{1,0:T(8,128)S(1)} %select_maximum_fusion), channel_id=1, source_target_pairs={{1,0},{0,1},{3,2},{2,3},{5,4},{4,5},{7,6},{6,7},{9,8},{8,9},{11,10... | collective-permute-start | bytes 208904 | tf_op jit(solution)/shard_map/ppermute | solution.py:306
  6.2 0.1 collective-permute-start.1
  6.2 1.6 %broadcast_select_fusion = (bf16[512,128]{1,0:T(8,128)(2,1)}, bf16[8,64,128]{2,1,0:T(8,128)(2,1)S(1)}) fusion(pred[]{:T(512)S(6)} %eq.13, f32[8,64,128]{2,1,0:T(8,128)} %param.6), kind=kLoop, calls=%fused_computation.12 | loop fusion | flops 131072 | bytes 524289 | tf_op jit(solution)/shard_map/jit(_where)/select_n | solution.py:332
  7.8 3.9 %collective-permute-start.2 = (bf16[512,128]{1,0:T(8,128)(2,1)S(1)}, bf16[512,128]{1,0:T(8,128)(2,1)S(1)}, u32[]{:S(2)}, u32[]{:S(2)}) collective-permute-start(bf16[512,128]{1,0:T(8,128)(2,1)S(1)} %bitcast.43), channel_id=1, source_target_pairs={{1,0},{0,1}} | collective-permute-start | bytes 393224 | tf_op jit(solution)/shard_map/ppermute | solution.py:327
  11.7 1.0 %slice.54 = bf16[3,8,64,128]{3,2,1,0:T(8,128)(2,1)S(1)} slice(bf16[4,8,64,128]{3,2,1,0:T(8,128)(2,1)} %param.7), slice={[0:3], [0:8], [0:64], [0:128]} | slice | bytes 786432 | tf_op jit(solution)/shard_map/slice | solution.py:324
  12.7 0.1 collective-permute-start.3
  12.9 0.8 copy.17
  13.7 0.8 tile.8
  14.5 0.3 tile.9
  14.8 0.0 copy-start.8
  14.8 0.2 copy.16
  15.0 1.5 %bitcast_convert_fusion = (bf16[1024,128]{1,0:T(8,128)(2,1)}, f32[128,1024]{0,1:T(8,128)S(1)}) fusion(f32[128,1024]{0,1:T(8,128)S(1)} %copy.16, s32[1024]{0:T(1024)S(1)} %get-tuple-element.41, s32[1024]{0:T(1024)S(1)} %get-tuple-element.42, pred[1024]{0:T(1024)(128)(4,1)S(1)} %fusion.9, s32[128]{0:T(128)S(1)} %get-tuple-element.43, ...), kind=kLoop, calls=%fused_computation.43 | loop fusion | flops 655360 | bytes 1321088 | tf_op jit(solution)/shard_map/convert_element_type | solution.py:373
  16.6 1.0 %copy.20.refs_3_.modes = f32[128,1024]{1,0:T(8,128)} copy(f32[128,1024]{0,1:T(8,128)S(1)} %get-tuple-element.33) | data formatting | bytes 1048576 | tf_op jit(solution)/shard_map/jit(_where)/select_n | solution.py:352
  17.6 0.6 pad_add_fusion.info
  18.1 0.0 collective-permute-done
  18.1 0.1 copy.18
  18.2 0.1 pad_maximum_fusion
  18.3 0.1 copy.19
  18.4 0.8 fusion.4.refs_4_
  19.1 0.6 concatenate.15.far_term
  19.8 0.0 copy-done.8
  19.8 0.6 add_select_fusion.nbr
  20.4 0.8 collective-permute-done.1.refs_1_
  21.2 0.0 copy-start.1
  21.2 0.8 copy-done.1
  22.0 16.9 %operator.1 = (bf16[1024,1024]{1,0:T(8,128)(2,1)}, bf16[4,512,128]{2,1,0:T(8,128)(2,1)}, f32[4,256,256]{2,1,0:T(8,128)}, f32[4,256,256]{2,1,0:T(8,128)}) custom-call(s32[4]{0:T(128)} %pad_add_fusion.info, s32[16,6]{1,0:T(8,128)} %add_select_fusion.nbr, bf16[8,64,448]{2,1,0:T(8,128)(2,1)} %refs_0_.1, bf16[8,64,448]{2,1,0:T(8,128)(2,1)} %copy-done.1, ...), custom_call_target="tpu_custom_call" | custom-call | tf_op jit(solution)/shard_map/operator/pallas_call | solution.py:357
  38.8 2.2 %slice_bitcast_fusion = (f32[256,256]{1,0:T(8,128)}, f32[256,256]{1,0:T(8,128)}, f32[256,256]{1,0:T(8,128)}, f32[256,256]{1,0:T(8,128)}) fusion(f32[4,256,256]{2,1,0:T(8,128)} %get-tuple-element.16), kind=kLoop, calls=%fused_computation.3 | loop fusion | bytes 2097152 | tf_op jit(solution)/shard_map/squeeze | solution.py:394
  41.0 0.0 copy-start
  41.0 0.0 collective-permute-done.2.refs_0_
  41.0 0.0 copy-start.7
  41.0 0.0 collective-permute-done.3.refs_1_
  41.0 0.0 copy-start.2
  41.1 0.6 copy-done.7
  41.7 0.1 copy-done.2
  41.8 7.8 %chain.1 = (f32[4,512,128]{2,1,0:T(8,128)}, f32[256,128]{1,0:T(8,128)}) custom-call(bf16[1024,1024]{1,0:T(8,128)(2,1)} %get-tuple-element.18.phi, bf16[512,128]{1,0:T(8,128)(2,1)} %get-tuple-element.30.first, bf16[4,512,128]{2,1,0:T(8,128)(2,1)} %bitcast.41, f32[128,1024]{1,0:T(8,128)} %copy.20.refs_3_.modes, f32[128,128]{1,0:T(8,128)} %concatenate.15.far_term, ...), custom_call_target="tpu_custom_call" | custom-call | tf_op jit(solution)/shard_map/chain/pallas_call | solution.py:375
  49.6 0.0 collective-permute-start.4
  49.6 0.0 copy-done
  49.6 0.9 %slice_bitcast_fusion.1 = (f32[256,256]{1,0:T(8,128)}, f32[256,256]{1,0:T(8,128)}, f32[256,256]{1,0:T(8,128)}) fusion(f32[4,256,256]{2,1,0:T(8,128)S(1)} %copy-done), kind=kLoop, calls=%fused_computation.4 | loop fusion | bytes 1572864 | tf_op jit(solution)/shard_map/squeeze | solution.py:394
  50.5 0.7 collective-permute-done.4.other
  51.2 0.0 copy-start.3
  51.2 0.7 broadcast_in_dim.21.before
  51.9 0.0 copy-done.3
  51.9 2.5 %join.3 = (f32[256,128]{1,0:T(8,128)}, f32[256,128]{1,0:T(8,128)}) custom-call(s32[1]{0:T(128)} %bitcast.bit, f32[256,256]{1,0:T(8,128)} %get-tuple-element.38.power.step, f32[256,256]{1,0:T(8,128)} %get-tuple-element.34.shift, f32[256,128]{1,0:T(8,128)} %get-tuple-element.19.mine.start, f32[256,128]{1,0:T(8,128)} %copy-done.3, ...), custom_call_target="tpu_custom_call" | custom-call | tf_op jit(solution)/shard_map/join/pallas_call | solution.py:388
  54.4 1.5 %collective-permute-start.5 = (f32[256,128]{1,0:T(8,128)}, f32[256,128]{1,0:T(8,128)S(1)}, u32[]{:S(2)}, u32[]{:S(2)}) collective-permute-start(f32[256,128]{1,0:T(8,128)} %get-tuple-element.20.mine), channel_id=1, source_target_pairs={{0,4},{2,6},{4,0},{6,2},{8,12},{10,14},{12,8},{14,10},{16,20},{18,... | collective-permute-start | bytes 393224 | tf_op jit(solution)/shard_map/ppermute | solution.py:386
  55.9 4.3 %collective-permute-done.5.other = f32[256,128]{1,0:T(8,128)S(1)} collective-permute-done((f32[256,128]{1,0:T(8,128)}, f32[256,128]{1,0:T(8,128)S(1)}, u32[]{:S(2)}, u32[]{:S(2)}) %collective-permute-start.5) | collective-permute-done | bytes 131104 | tf_op jit(solution)/shard_map/ppermute | solution.py:386
  60.1 0.0 copy-start.5
  60.1 0.7 copy-done.5
  60.8 2.5 %join.4 = (f32[256,128]{1,0:T(8,128)}, f32[256,128]{1,0:T(8,128)}) custom-call(s32[1]{0:T(128)} %bitcast.1.bit, f32[256,256]{1,0:T(8,128)} %get-tuple-element.39.power, f32[256,256]{1,0:T(8,128)} %get-tuple-element.35.shift, f32[256,128]{1,0:T(8,128)} %get-tuple-element.20.mine, f32[256,128]{1,0:T(8,128)} %copy-done.5, f32[256,128]{1,0:T(8,128)} %get-tuple-element.21.before), custom_call_target="tpu_custom_call" | custom-call | tf_op jit(solution)/shard_map/join/pallas_call | solution.py:388
  63.3 1.6 %collective-permute-start.6 = (f32[256,128]{1,0:T(8,128)}, f32[256,128]{1,0:T(8,128)S(1)}, u32[]{:S(2)}, u32[]{:S(2)}) collective-permute-start(f32[256,128]{1,0:T(8,128)} %get-tuple-element.22.mine), channel_id=1, source_target_pairs={{0,8},{2,10},{4,12},{6,14},{8,0},{10,2},{12,4},{14,6},{16,24},{18,... | collective-permute-start | bytes 393224 | tf_op jit(solution)/shard_map/ppermute | solution.py:386
  64.8 3.6 %collective-permute-done.6.other = f32[256,128]{1,0:T(8,128)S(1)} collective-permute-done((f32[256,128]{1,0:T(8,128)}, f32[256,128]{1,0:T(8,128)S(1)}, u32[]{:S(2)}, u32[]{:S(2)}) %collective-permute-start.6) | collective-permute-done | bytes 131104 | tf_op jit(solution)/shard_map/ppermute | solution.py:386
  68.4 0.0 copy-start.4
  68.4 0.7 copy-done.4
  69.1 2.5 %join.5 = (f32[256,128]{1,0:T(8,128)}, f32[256,128]{1,0:T(8,128)}) custom-call(s32[1]{0:T(128)} %bitcast.2.bit, f32[256,256]{1,0:T(8,128)} %get-tuple-element.40.power, f32[256,256]{1,0:T(8,128)} %get-tuple-element.36.shift, f32[256,128]{1,0:T(8,128)} %get-tuple-element.22.mine, f32[256,128]{1,0:T(8,128)} %copy-done.4, f32[256,128]{1,0:T(8,128)} %get-tuple-element.23.before), custom_call_target="tpu_custom_call" | custom-call | tf_op jit(solution)/shard_map/join/pallas_call | solution.py:388
  71.6 2.6 %collective-permute-start.7 = (f32[256,128]{1,0:T(8,128)}, f32[256,128]{1,0:T(8,128)S(1)}, u32[]{:S(2)}, u32[]{:S(2)}) collective-permute-start(f32[256,128]{1,0:T(8,128)} %get-tuple-element.24), channel_id=1, source_target_pairs={{0,16},{2,18},{4,20},{6,22},{8,24},{10,26},{12,28},{14,30},{16,0},... | collective-permute-start | bytes 393224 | tf_op jit(solution)/shard_map/ppermute | solution.py:386
  74.2 0.7 slice.60.modes_t
  74.9 4.2 %collective-permute-done.7.other = f32[256,128]{1,0:T(8,128)S(1)} collective-permute-done((f32[256,128]{1,0:T(8,128)}, f32[256,128]{1,0:T(8,128)S(1)}, u32[]{:S(2)}, u32[]{:S(2)}) %collective-permute-start.7) | collective-permute-done | bytes 131104 | tf_op jit(solution)/shard_map/ppermute | solution.py:386
  79.0 0.0 copy-start.6
  79.0 0.7 copy-done.6
  79.7 4.4 %last.1 = (f32[4,8,64,128]{3,2,1,0:T(8,128)}, f32[8,64,128]{2,1,0:T(8,128)}) custom-call(f32[256,256]{1,0:T(8,128)} %get-tuple-element.37.shift, f32[256,128]{1,0:T(8,128)} %copy-done.6, f32[256,128]{1,0:T(8,128)} %get-tuple-element.25.before, f32[256,256]{1,0:T(8,128)} %get-tuple-element.38.power.step, f32[256,128]{1,0:T(8,128)} %get-tuple-element.19.mine.start, ...), custom_call_target="tpu_custom_call" | custom-call | tf_op jit(solution)/shard_map/last/pallas_call | solution.py:395
  (8 shorter events, 0.0 us)
Async XLA Ops:
  3.2 15.0 %collective-permute-start = (f32[136,128]{1,0:T(8,128)S(1)}, f32[136,128]{1,0:T(8,128)S(1)}, u32[]{:S(2)}, u32[]{:S(2)}) collective-permute-start(f32[136,128]{1,0:T(8,128)S(1)} %select_maximum_fusion), channel_id=1, source_target_pairs={{1,0},{0,1},{3,2},{2,3},{5,4},{4,5},{7,6},{6,7},{9,8},{8,9},{11,10... | collective-permute-start | bytes 208904 | tf_op jit(solution)/shard_map/ppermute | solution.py:306
  6.2 15.0 %collective-permute-start.1 = (bf16[8,64,448]{2,1,0:T(8,128)(2,1)}, bf16[8,64,448]{2,1,0:T(8,128)(2,1)S(1)}, u32[]{:S(2)}, u32[]{:S(2)}) collective-permute-start(bf16[8,64,448]{2,1,0:T(8,128)(2,1)} %refs_0_.1), channel_id=1, source_target_pairs={{1,0},{0,1},{3,2},{2,3},{5,4},{4,5},{7,6},{6,7},{9,8},{8,9},{11,10... | collective-permute-start | bytes 1376264 | tf_op jit(solution)/shard_map/ppermute | solution.py:306
  7.8 33.2 %collective-permute-start.2 = (bf16[512,128]{1,0:T(8,128)(2,1)S(1)}, bf16[512,128]{1,0:T(8,128)(2,1)S(1)}, u32[]{:S(2)}, u32[]{:S(2)}) collective-permute-start(bf16[512,128]{1,0:T(8,128)(2,1)S(1)} %bitcast.43), channel_id=1, source_target_pairs={{1,0},{0,1}} | collective-permute-start | bytes 393224 | tf_op jit(solution)/shard_map/ppermute | solution.py:327
  12.7 28.3 %collective-permute-start.3 = (bf16[3,512,128]{2,1,0:T(8,128)(2,1)S(1)}, bf16[3,512,128]{2,1,0:T(8,128)(2,1)S(1)}, u32[]{:S(2)}, u32[]{:S(2)}) collective-permute-start(bf16[3,512,128]{2,1,0:T(8,128)(2,1)S(1)} %bitcast.42), channel_id=1, source_target_pairs={{1,0},{0,1},{3,2},{2,3},{5,4},{4,5},{7,6},{6,7},{9,8},{8,9},{11,10... | collective-permute-start | bytes 1179656 | tf_op jit(solution)/shard_map/ppermute | solution.py:306
  14.8 5.0 %copy-start.8 = (s32[8,6]{1,0:T(8,128)S(1)}, s32[8,6]{1,0:T(8,128)}, u32[]{:S(2)}) copy-start(s32[8,6]{1,0:T(8,128)} %param.9) | copy-start | bytes 580
  21.2 0.8 copy-start.1
  41.0 8.6 %copy-start = (f32[4,256,256]{2,1,0:T(8,128)S(1)}, f32[4,256,256]{2,1,0:T(8,128)}, u32[]{:S(2)}) copy-start(f32[4,256,256]{2,1,0:T(8,128)} %get-tuple-element.17) | copy-start | bytes 3145732
  41.0 0.7 copy-start.7
  41.0 0.8 copy-start.2
  49.6 1.6 %collective-permute-start.4 = (f32[256,128]{1,0:T(8,128)}, f32[256,128]{1,0:T(8,128)S(1)}, u32[]{:S(2)}, u32[]{:S(2)}) collective-permute-start(f32[256,128]{1,0:T(8,128)} %get-tuple-element.19.mine.start), channel_id=1, source_target_pairs={{0,2},{2,0},{4,6},{6,4},{8,10},{10,8},{12,14},{14,12},{16,18},{18,... | collective-permute-start | bytes 393224 | tf_op jit(solution)/shard_map/ppermute | solution.py:386
  51.2 0.7 copy-start.3
  54.4 5.8 %collective-permute-start.5 = (f32[256,128]{1,0:T(8,128)}, f32[256,128]{1,0:T(8,128)S(1)}, u32[]{:S(2)}, u32[]{:S(2)}) collective-permute-start(f32[256,128]{1,0:T(8,128)} %get-tuple-element.20.mine), channel_id=1, source_target_pairs={{0,4},{2,6},{4,0},{6,2},{8,12},{10,14},{12,8},{14,10},{16,20},{18,... | collective-permute-start | bytes 393224 | tf_op jit(solution)/shard_map/ppermute | solution.py:386
  60.1 0.7 copy-start.5
  63.3 5.2 %collective-permute-start.6 = (f32[256,128]{1,0:T(8,128)}, f32[256,128]{1,0:T(8,128)S(1)}, u32[]{:S(2)}, u32[]{:S(2)}) collective-permute-start(f32[256,128]{1,0:T(8,128)} %get-tuple-element.22.mine), channel_id=1, source_target_pairs={{0,8},{2,10},{4,12},{6,14},{8,0},{10,2},{12,4},{14,6},{16,24},{18,... | collective-permute-start | bytes 393224 | tf_op jit(solution)/shard_map/ppermute | solution.py:386
  68.4 0.7 copy-start.4
  71.6 7.5 %collective-permute-start.7 = (f32[256,128]{1,0:T(8,128)}, f32[256,128]{1,0:T(8,128)S(1)}, u32[]{:S(2)}, u32[]{:S(2)}) collective-permute-start(f32[256,128]{1,0:T(8,128)} %get-tuple-element.24), channel_id=1, source_target_pairs={{0,16},{2,18},{4,20},{6,22},{8,24},{10,26},{12,28},{14,30},{16,0},... | collective-permute-start | bytes 393224 | tf_op jit(solution)/shard_map/ppermute | solution.py:386
  79.0 0.7 copy-start.6

commit v2 on v0

--- a/solution.py
+++ b/solution.py
@@ -1,6 +1,10 @@
+import functools
+
 import jax
 import jax.numpy as jnp
 from jax import lax
+from jax.experimental import pallas as pl
+from jax.experimental.pallas import tpu as pltpu
 from jax.sharding import PartitionSpec as P
 
 BRICK = 64
@@ -9,9 +13,13 @@
 SWEEPS = 3
 STEPS = 4
 ITERS = 2
-
+GROUP = REACH
 
 highest = lax.Precision.HIGHEST
+f32 = jnp.float32
+bf16 = jnp.bfloat16
+VMEM = pl.BlockSpec(memory_space=pltpu.VMEM)
+SMEM = pl.BlockSpec(memory_space=pltpu.SMEM)
 
 
 def extended(block, sides, width):
@@ -67,7 +75,7 @@
     return jnp.mod(indices - position[:, None] + REACH, bricks_all) - REACH
 
 
-def body(initial, forcing, brick_blocks, neighbours, coarse_modes, coarse_blocks):
+def banded_body(initial, forcing, brick_blocks, neighbours, coarse_modes, coarse_blocks):
     bricks_here = initial.shape[0]
     bricks_all = bricks_here * lax.axis_size("space")
     first_brick = lax.axis_index("space") * bricks_here
@@ -121,6 +129,382 @@
     return (jnp.stack(outputs, 0), defect[None])
 
 
+def dot(a, b):
+    return jnp.dot(a, b, preferred_element_type=f32)
+
+
+def dot_f32(a, b):
+    return jnp.dot(a, b, preferred_element_type=f32, precision=highest)
+
+
+def high_low(a):
+    high = a.astype(bf16)
+    return high, (a - high.astype(f32)).astype(bf16)
+
+
+def dot_split(a, b):
+    a_high, a_low = high_low(a)
+    b_high, b_low = high_low(b)
+    return dot(a_high, b_high) + (dot(a_high, b_low) + dot(a_low, b_high))
+
+
+def call(kernel, name, out_shape, in_specs, *args, scratch=(), flops=0, vmem=16):
+    return pl.pallas_call(
+        kernel,
+        out_shape=out_shape,
+        in_specs=in_specs,
+        out_specs=jax.tree.map(lambda _: VMEM, out_shape),
+        scratch_shapes=scratch,
+        compiler_params=pltpu.CompilerParams(vmem_limit_bytes=vmem * 2 ** 20),
+        cost_estimate=pl.CostEstimate(flops=flops, bytes_accessed=2 ** 20, transcendentals=0),
+        name=name,
+    )(*args)
+
+
+def modes_kernel(modes, tall, both):
+    rows, size = tall.shape[0], tall.shape[1] // 2
+    bricks = size // Q
+    r = modes[...]
+    lane = lax.broadcasted_iota(jnp.int32, (Q, size), 1)
+    row = lax.broadcasted_iota(jnp.int32, (Q, size), 0)
+    pick = (lane % Q == row).astype(f32)
+    spread = lax.dot_general(
+        r, pick, (((0,), (0,)), ((), ())), preferred_element_type=f32, precision=highest
+    )
+    owner = lax.broadcasted_iota(jnp.int32, (BRICK, size), 1) // Q
+    for b in range(bricks):
+        high, low = high_low(jnp.where(owner == b, spread, 0.0))
+        tall[pl.ds(b * BRICK, BRICK), :size] = high
+        tall[pl.ds(b * BRICK, BRICK), size:] = low
+    gram = lax.dot_general(
+        r, r, (((1,), (1,)), ((), ())), preferred_element_type=f32, precision=highest
+    )
+    rest = r - dot_f32(gram, r)
+    for at, value in enumerate((r, rest)):
+        pair = jnp.concatenate([value, value], axis=1)
+        stack = jnp.concatenate([pair] * bricks, axis=0)
+        mine = lax.broadcasted_iota(jnp.int32, stack.shape, 0) // Q
+        half = lax.broadcasted_iota(jnp.int32, stack.shape, 1) // BRICK
+        for t in range(rows // 128):
+            both[pl.ds(at * size, size), pl.ds(t * 128, 128)] = jnp.where(
+                mine == 2 * t + half, stack, 0.0
+            ).astype(bf16)
+
+
+def operator_kernel(parts, info, nbr, own, *refs):
+    count = 2 * (parts - 1)
+    pieces = refs[:count]
+    first = refs[count]
+    far_first = refs[count + 1:count + parts]
+    tall, phi, state, off, diag, lin, masks = refs[count + parts:]
+    here = own.shape[0]
+    bricks = here * parts
+    groups = bricks // GROUP
+    span = GROUP * BRICK
+    lane = lax.broadcasted_iota(jnp.int32, (BRICK, 128), 1)
+    masks[0] = (lane < BRICK).astype(f32).astype(bf16)
+    masks[1] = (lane >= BRICK).astype(f32).astype(bf16)
+    off[...] = jnp.zeros_like(off)
+    diag[...] = jnp.zeros_like(diag)
+
+    def place_brick(source, r, b, in_group):
+        start = pl.multiple_of(b * BRICK, BRICK)
+        slots = source.shape[2] // BRICK
+        for s in range(slots):
+            width = min(128, source.shape[2] - (s // 2) * 128)
+            tile = source[r, :, pl.ds((s // 2) * 128, width)]
+            tile = tile[:, (s % 2) * BRICK:(s % 2 + 1) * BRICK]
+            double = jnp.concatenate([tile, tile], axis=1)
+            if s == 0:
+                diag[pl.ds(start, BRICK), pl.ds((in_group // 2) * 128, 128)] = (
+                    double * masks[in_group % 2]
+                )
+            else:
+                place = nbr[b, s - 1]
+                at = lax.div(place, 2)
+                off[at, pl.ds(start, BRICK), :] += double * masks[lax.rem(place, 2)]
+
+    for b in range(here):
+        place_brick(own, b, b, b % GROUP)
+    half = here // 2
+    core = info[0]
+    for p in range(parts - 1):
+        for j in range(half):
+            base = here * (p + 1) + j
+            place_brick(pieces[2 * p], j, base + half * core, j % GROUP)
+            place_brick(pieces[2 * p + 1], j, base + half * (1 - core), j % GROUP)
+
+    def near(r, k):
+        return (r - k) % groups in (0, 1, groups - 1)
+
+    for k in range(groups):
+        d = diag[pl.ds(k * span, span), :]
+        for r in range(groups):
+            if near(r, k):
+                o = jnp.concatenate(
+                    [off[k * (span // 128) + i, pl.ds(r * span, span), :] for i in range(span // 128)],
+                    axis=1,
+                )
+                lin[pl.ds(r * span, span), pl.ds(k * span, span)] = dot(o, d).astype(bf16)
+    for n in range(groups):
+        for r in range(groups):
+            acc = None
+            for k in range(groups):
+                if near(r, k) and near(k, n):
+                    part = dot(
+                        lin[pl.ds(r * span, span), pl.ds(k * span, span)],
+                        lin[pl.ds(k * span, span), pl.ds(n * span, span)],
+                    )
+                    acc = part if acc is None else acc + part
+            d = diag[pl.ds(r * span, span), :]
+            body = -acc if acc is not None else None
+            if near(r, n):
+                plain = lin[pl.ds(r * span, span), pl.ds(n * span, span)].astype(f32)
+                body = plain if body is None else plain + body
+            out = jnp.zeros((span, span), f32) if body is None else -dot(d, body.astype(bf16))
+            if r == n:
+                out = out + d.astype(f32)
+            phi[pl.ds(r * span, span), pl.ds(n * span, span)] = out.astype(bf16)
+    begin = jnp.concatenate([first[...]] + [r[...] for r in far_first], axis=0)
+    size = tall.shape[1] // 2
+    state[...] = dot(phi[...], jnp.concatenate([begin, tall[:, :size]], axis=1))
+
+
+def chain_kernel(parts, phi, state, force, both, far_term, *refs):
+    far_force = refs[:parts - 1]
+    iterates, images, start, coarse_phi = refs[parts - 1:]
+    own, ens = force.shape[1], force.shape[2]
+    full = state[...]
+    for i in range(STEPS):
+        mine = full[:own, :ens] + force[i].astype(f32)
+        iterates[i] = mine
+        moved = full[:, ens:].astype(bf16)
+        images[i] = moved[:own]
+        rows = [mine.astype(bf16)]
+        for p in range(parts - 1):
+            far = full[own * (p + 1):own * (p + 2), :ens]
+            if i < STEPS - 1:
+                far = far + far_force[p][i].astype(f32)
+            rows.append(far.astype(bf16))
+        current = jnp.concatenate([jnp.concatenate(rows, axis=0), moved], axis=1)
+        if i < STEPS - 1:
+            full = dot(phi[...], current)
+    got = dot(both[...], current)
+    size = got.shape[0] // 2
+    start[...] = got[:, :ens] + far_term[...]
+    coarse_phi[...] = got[:size, ens:]
+
+
+def recurrence_kernel(bits, info, modes, own_coarse, *refs):
+    far_coarse = refs[:-1 - bits]
+    coarse_phi = refs[-1 - bits]
+    outs = refs[-bits:]
+    size = coarse_phi.shape[0]
+    lane = lax.broadcasted_iota(jnp.int32, (Q, size), 1)
+    row = lax.broadcasted_iota(jnp.int32, (Q, size), 0)
+    pick = (lane % Q == row).astype(f32)
+    tall = jnp.concatenate([own_coarse[...]] + [r[...] for r in far_coarse], axis=0)
+    same = (
+        lax.broadcasted_iota(jnp.int32, (size, size), 0) // Q
+        == lax.broadcasted_iota(jnp.int32, (size, size), 1) // Q
+    )
+    a = jnp.where(same, dot_f32(tall, pick), 0.0)
+    r = modes[...]
+    gram = lax.dot_general(
+        r, r, (((1,), (1,)), ((), ())), preferred_element_type=f32, precision=highest
+    )
+    gram = jnp.where(same, jnp.concatenate([dot_f32(gram, pick)] * (size // Q), axis=0), 0.0)
+    lower = coarse_phi[...] - dot_f32(gram, a)
+    step = jnp.concatenate(
+        [
+            jnp.concatenate([a, jnp.zeros((size, size), f32)], axis=1),
+            jnp.concatenate([lower, a], axis=1),
+        ],
+        axis=0,
+    )
+    at = lax.broadcasted_iota(jnp.int32, step.shape, 0)
+    to = lax.broadcasted_iota(jnp.int32, step.shape, 1)
+    moved = (at == to).astype(f32)
+    for i in range(bits):
+        bit = info[1 + i] == 1
+        wide = 2 * size
+        high, low = high_low(step)
+        outs[i][pl.ds(0, wide), :wide] = high
+        outs[i][pl.ds(0, wide), wide:] = low
+        high, low = high_low(jnp.where(bit, moved, 0.0))
+        outs[i][pl.ds(wide, wide), :wide] = high
+        outs[i][pl.ds(wide, wide), wide:] = low
+        if i < bits - 1:
+            moved = jnp.where(bit, dot_split(moved, step), moved)
+            step = dot_split(step, step)
+
+
+def join_kernel(opening, info, powers, mine, other, *refs):
+    total, prefix = refs[-2:]
+    wide = mine.shape[0]
+    upper = info[0] == 1
+    own, came = mine[...].astype(bf16).astype(f32), other[...].astype(f32)
+    low = jnp.where(upper, came, own).astype(bf16)
+    high = jnp.where(upper, own, came)
+    moved = dot(powers[...], jnp.concatenate([low, low], axis=0))
+    total[...] = (moved[:wide] + high).astype(bf16)
+    if opening:
+        prefix[...] = moved[wide:]
+    else:
+        prefix[...] = refs[0][...] + moved[wide:]
+
+
+def last_kernel(powers, other, before, step, start, images, tall, iterates, solution, defect):
+    wide = before.shape[0]
+    size = wide // 2
+    shape = defect.shape
+    came = other[...]
+    prefix = before[...] + dot(powers[pl.ds(wide, wide), :], jnp.concatenate([came, came], axis=0))
+    low = prefix.astype(bf16)
+    mine = dot(step[pl.ds(0, wide), :], jnp.concatenate([low, low], axis=0)) + start[...]
+    first = mine[:size].astype(bf16)
+    both = (mine[:size] + mine[size:]).astype(bf16)
+    sum_low = (prefix[:size] + prefix[size:]).astype(bf16)
+    for i in range(STEPS - 1):
+        solution[i] = (iterates[i] + dot(images[i], sum_low)).reshape(shape)
+    m = tall[...]
+    solution[STEPS - 1] = dot(m, jnp.concatenate([both, both], axis=0)).reshape(shape)
+    defect[...] = (
+        iterates[STEPS - 1]
+        + dot(images[STEPS - 1], low[:size])
+        - dot(m, jnp.concatenate([first, first], axis=0))
+    ).reshape(shape)
+
+
+def dense_body(initial, forcing, brick_blocks, neighbours, coarse_modes, coarse_blocks):
+    here, _, ens = initial.shape
+    parts = lax.axis_size("space")
+    bricks = here * parts
+    own = here * BRICK
+    rows = bricks * BRICK
+    size = bricks * Q
+    slices = lax.axis_size("tm")
+    bits = slices.bit_length() - 1
+    first_brick = lax.axis_index("space") * here
+    place = lax.axis_index("tm")
+    sds = jax.ShapeDtypeStruct
+
+    def others(value):
+        return [
+            lax.ppermute(value, "space", [((s + k) % parts, s) for s in range(parts)])
+            for k in range(1, parts)
+        ]
+
+    def paired(value, bit):
+        return lax.ppermute(value, "tm", [(j, j ^ (1 << bit)) for j in range(slices)])
+
+    half = here // 2
+    core = place % 2
+    some = lax.dynamic_slice_in_dim(brick_blocks, core * half, half, axis=0)
+    fetched = others(some)
+    some, forcing = lax.optimization_barrier((some, forcing))
+    pieces = [piece for f in fetched for piece in (f, paired(f, 0))]
+    slots = neighbours.shape[1]
+    small = jnp.concatenate(
+        [
+            coarse_blocks.reshape(here * Q, Q),
+            jnp.pad(neighbours.astype(f32), ((0, 0), (0, Q - slots))),
+        ],
+        axis=0,
+    )
+    far_small = others(small)
+    force = forcing.reshape(STEPS, own, ens)
+    far_force = others(force[:STEPS - 1])
+    start_half = initial.astype(bf16).reshape(own, ens)
+    far_first = [
+        lax.ppermute(
+            start_half, ("tm", "space"), [((s + k) % parts, s) for s in range(parts)]
+        )
+        for k in range(1, parts)
+    ]
+    first = jnp.where(place == 0, start_half, jnp.zeros_like(start_half))
+    last_term = jnp.einsum(
+        "qc,bce->bqe", coarse_modes, forcing[STEPS - 1].astype(f32), precision=highest
+    )
+    gram = jnp.dot(coarse_modes, coarse_modes.T, precision=highest)
+    rest_term = last_term - jnp.einsum("qp,bpe->bqe", gram, last_term, precision=highest)
+    terms = jnp.stack([last_term, rest_term]).reshape(2, here * Q, ens)
+    far_terms = others(terms)
+    far_term = jnp.concatenate(
+        [jnp.zeros_like(terms)] + far_terms, axis=1
+    ).reshape(2 * size, ens)
+
+    nbr = jnp.concatenate(
+        [neighbours] + [f[here * Q:, :slots].astype(jnp.int32) for f in far_small], axis=0
+    )
+    nbr = jnp.mod(nbr - first_brick, bricks)
+    info = jnp.stack([core] + [(place >> i) & 1 for i in range(bits)]).astype(jnp.int32)
+
+    tall, both = call(
+        modes_kernel,
+        "modes",
+        (sds((rows, 2 * size), bf16), sds((2 * size, rows), bf16)),
+        [VMEM],
+        coarse_modes,
+    )
+    phi, state = call(
+        functools.partial(operator_kernel, parts),
+        "operator",
+        (sds((rows, rows), bf16), sds((rows, ens + size), f32)),
+        [SMEM, SMEM] + [VMEM] * (3 * parts),
+        info, nbr, brick_blocks, *pieces, first, *far_first, tall,
+        scratch=[
+            pltpu.VMEM((rows // 128, rows, 128), bf16),
+            pltpu.VMEM((rows, GROUP * BRICK), bf16),
+            pltpu.VMEM((rows, rows), bf16),
+            pltpu.VMEM((2, BRICK, 128), bf16),
+        ],
+        flops=2 * 4 * rows * rows * ens,
+    )
+    iterates, images, start, coarse_phi = call(
+        functools.partial(chain_kernel, parts),
+        "chain",
+        (
+            sds((STEPS, own, ens), f32),
+            sds((STEPS, own, size), bf16),
+            sds((2 * size, ens), f32),
+            sds((size, size), f32),
+        ),
+        [VMEM] * (4 + parts),
+        phi, state, force, both, far_term, *far_force,
+        flops=2 * 3 * rows * rows * (ens + size),
+    )
+    powers = call(
+        functools.partial(recurrence_kernel, bits),
+        "recurrence",
+        tuple(sds((4 * size, 4 * size), bf16) for _ in range(bits)),
+        [SMEM] + [VMEM] * (2 + parts),
+        info, coarse_modes, coarse_blocks.reshape(here * Q, Q),
+        *[f[:here * Q] for f in far_small], coarse_phi,
+        flops=2 * 9 * (2 * size) ** 3,
+    )
+    total = start.astype(bf16)
+    prefix = None
+    for i in range(bits):
+        other = paired(total, i)
+        if i < bits - 1:
+            total, prefix = call(
+                functools.partial(join_kernel, prefix is None),
+                "join",
+                (sds((2 * size, ens), bf16), sds((2 * size, ens), f32)),
+                [SMEM] + [VMEM] * (3 if prefix is None else 4),
+                info[i + 1:i + 2], powers[i], total, other, *(() if prefix is None else (prefix,)),
+            )
+    solution_out, defect = call(
+        last_kernel,
+        "last",
+        (sds((STEPS, here, BRICK, ens), f32), sds((here, BRICK, ens), f32)),
+        [VMEM] * 8,
+        powers[bits - 1], other, prefix, powers[0], start, images, tall[:own], iterates,
+    )
+    return solution_out, defect[None]
+
+
 def solution(mesh):
     placed = (
         P("space", None, None),
@@ -130,6 +514,15 @@
         P(),
         P("space", None, None),
     )
+
+    def body(initial, *rest):
+        here = initial.shape[0]
+        bricks = here * lax.axis_size("space")
+        slices = lax.axis_size("tm")
+        fits = 8 * (bricks * BRICK) ** 2 <= 16 * 2 ** 20
+        even = here % (2 * GROUP) == 0 and slices > 2 and slices & (slices - 1) == 0
+        return (dense_body if fits and even else banded_body)(initial, *rest)
+
     return jax.shard_map(
         body,
         mesh=mesh,

time: 260 us -> 50.1 us (0.19)
  the two profiles are of different devices: /device:TPU:26 before, /device:TPU:0 now
where the time goes in v2:
time: 50.1 us; the launch traced here: 49.7 us
  waiting for transfers between devices  16.3 us (33%)
  Pallas kernels  16.2 us (32%)
  starting transfers between devices  9.45 us (19%)
  other arithmetic  2.52 us (5%)
  local copies, waits for them, and re-layouts  2.14 us (4%)
  matrix products  2.13 us (4%)
  between operations  0.91 us (2%)
    pallas_call x8, Pallas kernels, call(): pl.pallas_call(kernel, out_shape=out_shape, in_specs=in_specs, out_specs=...  16.2 us
    ppermute x5, waiting for transfers between devices, paired(): return lax.ppermute(value, 'tm', [(j, j ^ 1 << bit) for j in range(slices)])  14 us
    ppermute x4, starting transfers between devices, others(): lax.ppermute(value, 'space', [((s + k) % parts, s) for s in range(parts)])  7.21 us
    ppermute x1, waiting for transfers between devices, dense_body(): lax.ppermute(start_half, ('tm', 'space'), [((s + k) % parts, s) for s in...  2.32 us
    ppermute x1, starting transfers between devices, dense_body(): lax.ppermute(start_half, ('tm', 'space'), [((s + k) % parts, s) for s in...  1.94 us
    dot_general x1, matrix products, dense_body(): jnp.einsum('qc,bce->bqe', coarse_modes, forcing[STEPS - 1].astype(f32), p...  1.08 us
    slice x1, local copies, waits for them, and re-layouts, dense_body(): far_force = others(force[:STEPS - 1])  1.02 us
  transfers between devices with their start and end apart: 10, of which 4 were waited for; matrix products, arithmetic and copies ran while one was open for 11% of the time, Pallas kernels for 21%

profile of v2, /device:TPU:0, one launch (start us, length us, event | category | flops | bytes accessed | tf_op | source)
XLA Modules:
  0.0 49.7 jit_solution(10843920701190124016)
XLA Ops:
  0.6 0.0 copy-start.4
  0.6 0.0 copy-start.1
  0.7 0.0 copy-start.2
  0.7 0.8 %convert_element_type.15 = f32[8,6]{1,0:T(8,128)S(1)} convert(s32[8,6]{1,0:T(8,128)} %param.9) | non-fusion elementwise | flops 48 | bytes 384 | tf_op jit(solution)/shard_map/convert_element_type | solution.py:411
  1.4 0.8 %select_maximum_fusion = f32[72,8]{1,0:T(8,128)S(1)} fusion(f32[8,6]{1,0:T(8,128)S(1)} %convert_element_type.15, f32[64,8]{1,0:T(8,128)} %bitcast.38), kind=kLoop, calls=%fused_computation.9 | loop fusion | flops 1728 | bytes 4544 | tf_op jit(solution)/shard_map/concatenate | solution.py:408
  2.2 3.0 %collective-permute-start = (f32[72,8]{1,0:T(8,128)S(1)}, f32[72,8]{1,0:T(8,128)S(1)}, u32[]{:S(2)}, u32[]{:S(2)}) collective-permute-start(f32[72,8]{1,0:T(8,128)S(1)} %select_maximum_fusion), channel_id=1, source_target_pairs={{1,0},{0,1},{3,2},{2,3},{5,4},{4,5},{7,6},{6,7},{9,8},{8,9},{11,10... | collective-permute-start | bytes 6920 | tf_op jit(solution)/shard_map/ppermute | solution.py:394
  5.2 1.0 %constant_dynamic-slice_fusion = bf16[4,64,448]{2,1,0:T(8,128)(2,1)S(1)} fusion(bf16[8,64,448]{2,1,0:T(8,128)(2,1)} %own.1, s32[]{:T(128)S(6)} %select_n.26), kind=kLoop, calls=%fused_computation.19 | loop fusion | bytes 458756 | tf_op jit(solution)/shard_map/dynamic_slice | solution.py:403
  6.1 0.1 collective-permute-start.1
  6.2 0.9 %convolution_bitcast_fusion.1 = f32[8,8,1]{1,0,2:T(8,128)S(1)} fusion(f32[8,64]{1,0:T(8,128)} %modes.5), kind=kOutput, calls=%fused_computation.3 | convolution fusion | flops 49152 | bytes 2304 | tf_op jit(solution)/shard_map/dot_general | solution.py:429
  7.1 1.1 %fusion.2 = f32[8,128,8]{1,2,0:T(8,128)S(1)} fusion(bf16[4,8,64,128]{3,2,1,0:T(8,128)(2,1)} %param.7, f32[8,64]{1,0:T(8,128)} %modes.5), kind=kOutput, calls=%fused_computation.4 | convolution fusion | flops 6291456 | bytes 167936 | tf_op jit(solution)/shard_map/qc,bce->bqe/dot_general | solution.py:426
  8.2 0.2 fusion.1
  8.4 2.1 %collective-permute-start.4 = (f32[2,64,128]{2,1,0:T(8,128)S(1)}, f32[2,64,128]{2,1,0:T(8,128)S(1)}, u32[]{:S(2)}, u32[]{:S(2)}) collective-permute-start(f32[2,64,128]{2,1,0:T(8,128)S(1)} %pad_maximum_fusion), channel_id=1, source_target_pairs={{1,0},{0,1},{3,2},{2,3},{5,4},{4,5},{7,6},{6,7},{9,8},{8,9},{11,10... | collective-permute-start | bytes 196616 | tf_op jit(solution)/shard_map/ppermute | solution.py:394
  10.5 1.0 %broadcast_select_fusion = (bf16[512,128]{1,0:T(8,128)(2,1)S(1)}, bf16[8,64,128]{2,1,0:T(8,128)(2,1)S(1)}) fusion(pred[]{:T(512)S(6)} %eq.7, f32[8,64,128]{2,1,0:T(8,128)} %param.6), kind=kLoop, calls=%fused_computation.7 | loop fusion | flops 131072 | bytes 524289 | tf_op jit(solution)/shard_map/jit(_where)/select_n | solution.py:425
  11.4 1.9 %collective-permute-start.3 = (bf16[512,128]{1,0:T(8,128)(2,1)S(1)}, bf16[512,128]{1,0:T(8,128)(2,1)S(1)}, u32[]{:S(2)}, u32[]{:S(2)}) collective-permute-start(bf16[512,128]{1,0:T(8,128)(2,1)S(1)} %bitcast.42), channel_id=1, source_target_pairs={{1,0},{0,1}} | collective-permute-start | bytes 393224 | tf_op jit(solution)/shard_map/ppermute | solution.py:420
  13.4 1.0 %slice.21 = bf16[3,8,64,128]{3,2,1,0:T(8,128)(2,1)S(1)} slice(bf16[4,8,64,128]{3,2,1,0:T(8,128)(2,1)} %param.7), slice={[0:3], [0:8], [0:64], [0:128]} | slice | bytes 786432 | tf_op jit(solution)/shard_map/slice | solution.py:417
  14.4 2.1 %collective-permute-start.5 = (bf16[3,512,128]{2,1,0:T(8,128)(2,1)S(1)}, bf16[3,512,128]{2,1,0:T(8,128)(2,1)S(1)}, u32[]{:S(2)}, u32[]{:S(2)}) collective-permute-start(bf16[3,512,128]{2,1,0:T(8,128)(2,1)S(1)} %bitcast.40), channel_id=1, source_target_pairs={{1,0},{0,1},{3,2},{2,3},{5,4},{4,5},{7,6},{6,7},{9,8},{8,9},{11,10... | collective-permute-start | bytes 1179656 | tf_op jit(solution)/shard_map/ppermute | solution.py:394
  16.5 0.0 copy-done.2
  16.5 0.7 %modes.3 = (bf16[1024,256]{1,0:T(8,128)(2,1)S(1)}, bf16[256,1024]{1,0:T(8,128)(2,1)S(1)}) custom-call(f32[8,64]{1,0:T(8,128)S(1)} %copy-done.2), custom_call_target="tpu_custom_call" | custom-call | bytes 1048576 | tf_op jit(solution)/shard_map/modes/pallas_call | solution.py:152
  17.2 0.1 stack.32.info
  17.3 0.0 collective-permute-done.1.refs_0_
  17.3 0.0 collective-permute-start.2
  17.3 0.0 collective-permute-done
  17.3 0.0 copy-done.4
  17.3 0.0 copy-start
  17.3 0.0 collective-permute-done.4
  17.4 2.3 %collective-permute-done.3.refs_3_ = bf16[512,128]{1,0:T(8,128)(2,1)S(1)} collective-permute-done((bf16[512,128]{1,0:T(8,128)(2,1)S(1)}, bf16[512,128]{1,0:T(8,128)(2,1)S(1)}, u32[]{:S(2)}, u32[]{:S(2)}) %collective-permute-start.3) | collective-permute-done | bytes 131104 | tf_op jit(solution)/shard_map/ppermute | solution.py:420
  19.7 0.0 collective-permute-done.2.refs_1_
  19.7 0.0 copy-done.1
  19.7 7.7 %operator.1 = (bf16[1024,1024]{1,0:T(8,128)(2,1)S(1)}, f32[1024,256]{1,0:T(8,128)S(1)}) custom-call(s32[5]{0:T(128)S(1)} %stack.32.info, s32[16,6]{1,0:T(8,128)S(1)} %add_select_fusion.nbr, bf16[8,64,448]{2,1,0:T(8,128)(2,1)S(1)} %copy-done.1, bf16[4,64,448]{2,1,0:T(8,128)(2,1)S(1)} %collective-permute-done.1.refs_0_, ...), custom_call_target="tpu_custom_call" | custom-call | flops 1073741824 | bytes 1048576 | tf_op jit(solution)/shard_map/operator/pallas_call | solution.py:152
  27.4 0.0 collective-permute-done.5.refs_0_
  27.5 0.0 copy-done
  27.5 0.0 copy-start.3
  27.5 3.0 %chain.1 = (f32[4,512,128]{2,1,0:T(8,128)S(1)}, bf16[4,512,128]{2,1,0:T(8,128)(2,1)S(1)}, f32[256,128]{1,0:T(8,128)S(1)}, f32[128,128]{1,0:T(8,128)S(1)}) custom-call(bf16[1024,1024]{1,0:T(8,128)(2,1)S(1)} %get-tuple-element.24.phi, f32[1024,256]{1,0:T(8,128)S(1)} %get-tuple-element.25.state, bf16[4,512,128]{2,1,0:T(8,128)(2,1)S(1)} %bitcast.36, ...), custom_call_target="tpu_custom_call" | custom-call | flops 1610612736 | bytes 1048576 | tf_op jit(solution)/shard_map/chain/pallas_call | solution.py:152
  30.5 0.1 collective-permute-start.6
  30.6 0.0 copy-done.3
  30.6 2.1 %recurrence.1 = (bf16[512,512]{1,0:T(8,128)(2,1)S(1)}, bf16[512,512]{1,0:T(8,128)(2,1)S(1)}, bf16[512,512]{1,0:T(8,128)(2,1)S(1)}, bf16[512,512]{1,0:T(8,128)(2,1)S(1)}) custom-call(s32[5]{0:T(128)S(1)} %stack.32.info, f32[8,64]{1,0:T(8,128)S(1)} %copy-done.2, f32[64,8]{1,0:T(8,128)S(1)} %bitcast.39, f32[64,8]{1,0:T(8,128)S(1)} %slice.24.refs_0_, ...), custom_call_target="tpu_custom_call" | custom-call | flops 301989888 | bytes 1048576 | tf_op jit(solution)/shard_map/recurrence/pallas_call | solution.py:152
  32.7 0.0 collective-permute-done.6.other
  32.7 0.3 join.3
  33.1 0.1 collective-permute-start.7
  33.1 4.5 %collective-permute-done.7.other = bf16[256,128]{1,0:T(8,128)(2,1)S(1)} collective-permute-done((bf16[256,128]{1,0:T(8,128)(2,1)S(1)}, bf16[256,128]{1,0:T(8,128)(2,1)S(1)}, u32[]{:S(2)}, u32[]{:S(2)}) %collective-permute-start.7) | collective-permute-done | bytes 65568 | tf_op jit(solution)/shard_map/ppermute | solution.py:399
  37.6 0.3 join.4
  37.9 0.1 collective-permute-start.8
  38.0 4.3 %collective-permute-done.8.other = bf16[256,128]{1,0:T(8,128)(2,1)S(1)} collective-permute-done((bf16[256,128]{1,0:T(8,128)(2,1)S(1)}, bf16[256,128]{1,0:T(8,128)(2,1)S(1)}, u32[]{:S(2)}, u32[]{:S(2)}) %collective-permute-start.8) | collective-permute-done | bytes 65568 | tf_op jit(solution)/shard_map/ppermute | solution.py:399
  42.2 0.3 join.5
  42.5 0.1 collective-permute-start.9
  42.6 5.3 %collective-permute-done.9.other = bf16[256,128]{1,0:T(8,128)(2,1)S(1)} collective-permute-done((bf16[256,128]{1,0:T(8,128)(2,1)S(1)}, bf16[256,128]{1,0:T(8,128)(2,1)S(1)}, u32[]{:S(2)}, u32[]{:S(2)}) %collective-permute-start.9) | collective-permute-done | bytes 65568 | tf_op jit(solution)/shard_map/ppermute | solution.py:399
  47.9 1.8 %last.1 = (f32[4,8,64,128]{3,2,1,0:T(8,128)}, f32[8,64,128]{2,1,0:T(8,128)}) custom-call(bf16[512,512]{1,0:T(8,128)(2,1)S(1)} %get-tuple-element.29.powers, bf16[256,128]{1,0:T(8,128)(2,1)S(1)} %collective-permute-done.9.other, f32[256,128]{1,0:T(8,128)S(1)} %get-tuple-element.39.before, bf16[512,512]{1,0:T(8,128)(2,1)S(1)} %get-tuple-element.32.powers.step, ...), custom_call_target="tpu_custom_call" | custom-call | bytes 1048576 | tf_op jit(solution)/shard_map/last/pallas_call | solution.py:152
  (7 shorter events, 0.1 us)
Async XLA Ops:
  0.6 16.7 %copy-start.4 = (s32[8,6]{1,0:T(8,128)S(1)}, s32[8,6]{1,0:T(8,128)}, u32[]{:S(2)}) copy-start(s32[8,6]{1,0:T(8,128)} %param.9) | copy-start | bytes 580
  0.6 19.1 %copy-start.1 = (bf16[8,64,448]{2,1,0:T(8,128)(2,1)S(1)}, bf16[8,64,448]{2,1,0:T(8,128)(2,1)}, u32[]{:S(2)}) copy-start(bf16[8,64,448]{2,1,0:T(8,128)(2,1)} %own.1) | copy-start | bytes 1376260
  0.7 15.8 %copy-start.2 = (f32[8,64]{1,0:T(8,128)S(1)}, f32[8,64]{1,0:T(8,128)}, u32[]{:S(2)}) copy-start(f32[8,64]{1,0:T(8,128)} %modes.5) | copy-start | bytes 6148
  2.2 15.1 %collective-permute-start = (f32[72,8]{1,0:T(8,128)S(1)}, f32[72,8]{1,0:T(8,128)S(1)}, u32[]{:S(2)}, u32[]{:S(2)}) collective-permute-start(f32[72,8]{1,0:T(8,128)S(1)} %select_maximum_fusion), channel_id=1, source_target_pairs={{1,0},{0,1},{3,2},{2,3},{5,4},{4,5},{7,6},{6,7},{9,8},{8,9},{11,10... | collective-permute-start | bytes 6920 | tf_op jit(solution)/shard_map/ppermute | solution.py:394
  6.1 11.1 %collective-permute-start.1 = (bf16[4,64,448]{2,1,0:T(8,128)(2,1)S(1)}, bf16[4,64,448]{2,1,0:T(8,128)(2,1)S(1)}, u32[]{:S(2)}, u32[]{:S(2)}) collective-permute-start(bf16[4,64,448]{2,1,0:T(8,128)(2,1)S(1)} %constant_dynamic-slice_fusion), channel_id=1, source_target_pairs={{1,0},{0,1},{3,2},{2,3},{5,4},{4,5},{7,6},{6,7},{9,8},{8,9},{11,10... | collective-permute-start | bytes 688136 | tf_op jit(solution)/shard_map/ppermute | solution.py:394
  8.4 9.0 %collective-permute-start.4 = (f32[2,64,128]{2,1,0:T(8,128)S(1)}, f32[2,64,128]{2,1,0:T(8,128)S(1)}, u32[]{:S(2)}, u32[]{:S(2)}) collective-permute-start(f32[2,64,128]{2,1,0:T(8,128)S(1)} %pad_maximum_fusion), channel_id=1, source_target_pairs={{1,0},{0,1},{3,2},{2,3},{5,4},{4,5},{7,6},{6,7},{9,8},{8,9},{11,10... | collective-permute-start | bytes 196616 | tf_op jit(solution)/shard_map/ppermute | solution.py:394
  11.4 8.3 %collective-permute-start.3 = (bf16[512,128]{1,0:T(8,128)(2,1)S(1)}, bf16[512,128]{1,0:T(8,128)(2,1)S(1)}, u32[]{:S(2)}, u32[]{:S(2)}) collective-permute-start(bf16[512,128]{1,0:T(8,128)(2,1)S(1)} %bitcast.42), channel_id=1, source_target_pairs={{1,0},{0,1}} | collective-permute-start | bytes 393224 | tf_op jit(solution)/shard_map/ppermute | solution.py:420
  14.4 13.0 %collective-permute-start.5 = (bf16[3,512,128]{2,1,0:T(8,128)(2,1)S(1)}, bf16[3,512,128]{2,1,0:T(8,128)(2,1)S(1)}, u32[]{:S(2)}, u32[]{:S(2)}) collective-permute-start(bf16[3,512,128]{2,1,0:T(8,128)(2,1)S(1)} %bitcast.40), channel_id=1, source_target_pairs={{1,0},{0,1},{3,2},{2,3},{5,4},{4,5},{7,6},{6,7},{9,8},{8,9},{11,10... | collective-permute-start | bytes 1179656 | tf_op jit(solution)/shard_map/ppermute | solution.py:394
  17.3 2.4 %collective-permute-start.2 = (bf16[4,64,448]{2,1,0:T(8,128)(2,1)S(1)}, bf16[4,64,448]{2,1,0:T(8,128)(2,1)S(1)}, u32[]{:S(2)}, u32[]{:S(2)}) collective-permute-start(bf16[4,64,448]{2,1,0:T(8,128)(2,1)S(1)} %collective-permute-done.1.refs_0_), channel_id=1, source_target_pairs={{0,2},{2,0},{4,6},{6,4},{8,10},{10,8},{12,14},{14,12},{16,18},{18,... | collective-permute-start | bytes 688136 | tf_op jit(solution)/shard_map/ppermute | solution.py:399
  17.3 10.1 %copy-start = (bf16[4,8,64,128]{3,2,1,0:T(8,128)(2,1)S(1)}, bf16[4,8,64,128]{3,2,1,0:T(8,128)(2,1)}, u32[]{:S(2)}) copy-start(bf16[4,8,64,128]{3,2,1,0:T(8,128)(2,1)} %param.7) | copy-start | bytes 1572868
  27.5 3.1 %copy-start.3 = (f32[8,8,8]{2,1,0:T(8,128)S(1)}, f32[8,8,8]{2,1,0:T(8,128)}, u32[]{:S(2)}) copy-start(f32[8,8,8]{2,1,0:T(8,128)} %param.11) | copy-start | bytes 6148
  30.5 2.2 %collective-permute-start.6 = (bf16[256,128]{1,0:T(8,128)(2,1)S(1)}, bf16[256,128]{1,0:T(8,128)(2,1)S(1)}, u32[]{:S(2)}, u32[]{:S(2)}) collective-permute-start(bf16[256,128]{1,0:T(8,128)(2,1)S(1)} %convert_element_type.18.mine), channel_id=1, source_target_pairs={{0,2},{2,0},{4,6},{6,4},{8,10},{10,8},{12,14},{14,12},{16,18},{18,... | collective-permute-start | bytes 196616 | tf_op jit(solution)/shard_map/ppermute | solution.py:399
  33.1 4.5 %collective-permute-start.7 = (bf16[256,128]{1,0:T(8,128)(2,1)S(1)}, bf16[256,128]{1,0:T(8,128)(2,1)S(1)}, u32[]{:S(2)}, u32[]{:S(2)}) collective-permute-start(bf16[256,128]{1,0:T(8,128)(2,1)S(1)} %get-tuple-element.34.mine), channel_id=1, source_target_pairs={{0,4},{2,6},{4,0},{6,2},{8,12},{10,14},{12,8},{14,10},{16,20},{18,... | collective-permute-start | bytes 196616 | tf_op jit(solution)/shard_map/ppermute | solution.py:399
  37.9 4.3 %collective-permute-start.8 = (bf16[256,128]{1,0:T(8,128)(2,1)S(1)}, bf16[256,128]{1,0:T(8,128)(2,1)S(1)}, u32[]{:S(2)}, u32[]{:S(2)}) collective-permute-start(bf16[256,128]{1,0:T(8,128)(2,1)S(1)} %get-tuple-element.36.mine), channel_id=1, source_target_pairs={{0,8},{2,10},{4,12},{6,14},{8,0},{10,2},{12,4},{14,6},{16,24},{18,... | collective-permute-start | bytes 196616 | tf_op jit(solution)/shard_map/ppermute | solution.py:399
  42.5 5.4 %collective-permute-start.9 = (bf16[256,128]{1,0:T(8,128)(2,1)S(1)}, bf16[256,128]{1,0:T(8,128)(2,1)S(1)}, u32[]{:S(2)}, u32[]{:S(2)}) collective-permute-start(bf16[256,128]{1,0:T(8,128)(2,1)S(1)} %get-tuple-element.38), channel_id=1, source_target_pairs={{0,16},{2,18},{4,20},{6,22},{8,24},{10,26},{12,28},{14,30},{16,0},... | collective-permute-start | bytes 196616 | tf_op jit(solution)/shard_map/ppermute | solution.py:399

commit v3 on v2

v3 whole, which is shorter than its diff:
```python
import functools

import jax
import jax.numpy as jnp
from jax import lax
from jax.experimental import pallas as pl
from jax.experimental.pallas import tpu as pltpu
from jax.sharding import PartitionSpec as P


BRICK = 64
REACH = 4
Q = 8
SWEEPS = 3
STEPS = 4
ITERS = 2
GROUP = REACH

highest = lax.Precision.HIGHEST
f32 = jnp.float32
bf16 = jnp.bfloat16
VMEM = pl.BlockSpec(memory_space=pltpu.VMEM)
SMEM = pl.BlockSpec(memory_space=pltpu.SMEM)
HBM = pl.BlockSpec(memory_space=pltpu.HBM)


def extended(block, sides, width):
    for axis, dim in sides:
        count = lax.axis_size(axis)
        forward = [(i, i + 1) for i in range(count - 1)]
        forward.append((count - 1, 0))
        backward = [(target, source) for source, target in forward]
        low = lax.ppermute(
            lax.slice_in_dim(block, block.shape[dim] - width, None, axis=dim), axis, forward
        )
        high = lax.ppermute(lax.slice_in_dim(block, 0, width, axis=dim), axis, backward)
        block = jnp.concatenate([low, block, high], axis=dim)
    return block


def carried_in(part, axis, combine, identity):
    place = lax.axis_index(axis)
    gathered = jax.tree.map(lambda a: lax.all_gather(a, axis), part)
    state = jax.tree.map(lambda a, e: jnp.zeros_like(a) + jnp.asarray(e, a.dtype), part, identity)

    def one(turn, state):
        return combine(
            state, jax.tree.map(lambda a: lax.dynamic_index_in_dim(a, turn, 0, False), gathered)
        )

    return lax.fori_loop(0, place, one, state)


def from_behind(block, axis, distance):
    devices = range(lax.axis_size(axis))
    route = [(i - distance, i) for i in devices if i - distance in devices]
    return lax.ppermute(block, axis, route)


def apply_inverse(diag_blocks, values):
    return jnp.einsum(
        "bij,bje->bie", diag_blocks, values.astype(jnp.bfloat16), preferred_element_type=jnp.float32
    )


def coupling(off_blocks, source, positions):
    picked = jnp.take(source, positions, axis=0)
    merged = picked.reshape(
        positions.shape[0], positions.shape[1] * source.shape[1], source.shape[2]
    )
    return jnp.einsum("bim,bme->bie", off_blocks, merged, preferred_element_type=jnp.float32)


def wrapped_offsets(indices, first_row, bricks_all):
    row_ids = jnp.arange(indices.shape[0], dtype=jnp.int32)
    position = jnp.mod(first_row + row_ids, bricks_all)
    return jnp.mod(indices - position[:, None] + REACH, bricks_all) - REACH


def banded_body(initial, forcing, brick_blocks, neighbours, coarse_modes, coarse_blocks):
    bricks_here = initial.shape[0]
    bricks_all = bricks_here * lax.axis_size("space")
    first_brick = lax.axis_index("space") * bricks_here
    slice_index = lax.axis_index("tm")
    own_shifts = wrapped_offsets(neighbours, first_brick, bricks_all)
    where_from = jnp.arange(bricks_here, dtype=jnp.int32)[:, None] + REACH + own_shifts
    diagonal = brick_blocks[:, :, :BRICK]
    off_blocks = brick_blocks[:, :, BRICK:]

    def propagate(values):
        iterate = apply_inverse(diagonal, values)
        for _ in range(1, SWEEPS):
            rimmed = extended(iterate.astype(jnp.bfloat16), (("space", 0),), REACH)
            iterate = apply_inverse(diagonal, values - coupling(off_blocks, rimmed, where_from))
        return iterate

    is_first = slice_index == 0
    slice_starts = jnp.where(is_first, initial, jnp.zeros_like(initial))
    slice_ends = jnp.zeros_like(initial)
    identity = jnp.broadcast_to(jnp.eye(Q, dtype=jnp.float32), coarse_blocks.shape)
    nothing = jnp.zeros((bricks_here, Q, initial.shape[2]), jnp.float32)

    def compose(earlier, later):
        matrix = jnp.einsum("bpq,bqr->bpr", later[0], earlier[0], precision=highest)
        offset = jnp.einsum("bpq,bqe->bpe", later[0], earlier[1], precision=highest) + later[1]
        return (matrix, offset)

    defect = slice_ends
    for _ in range(ITERS):
        current = slice_starts
        for substep in range(STEPS - 1):
            current = propagate(current) + forcing[substep].astype(jnp.float32)
        defect = propagate(current) + forcing[STEPS - 1].astype(jnp.float32) - slice_ends
        restricted = jnp.einsum("qc,bce->bqe", coarse_modes, defect, precision=highest)
        prefix = carried_in((coarse_blocks, restricted), "tm", compose, (identity, nothing))
        before = prefix[1]
        corrected = (
            jnp.einsum("bpq,bqe->bpe", coarse_blocks, before, precision=highest) + restricted
        )
        slice_ends = slice_ends + jnp.einsum(
            "qc,bqe->bce", coarse_modes, corrected, precision=highest
        )
        shifted = from_behind(slice_ends.astype(jnp.bfloat16), "tm", 1).astype(slice_ends.dtype)
        slice_starts = jnp.where(is_first, initial, shifted)
    outputs = []
    current = slice_starts
    for substep in range(STEPS - 1):
        current = propagate(current) + forcing[substep].astype(jnp.float32)
        outputs.append(current)
    outputs.append(slice_ends)
    return (jnp.stack(outputs, 0), defect[None])


def dot(a, b):
    return jnp.dot(a, b, preferred_element_type=f32)


def dot_f32(a, b):
    return jnp.dot(a, b, preferred_element_type=f32, precision=highest)


def high_low(a):
    high = a.astype(bf16)
    return high, (a - high.astype(f32)).astype(bf16)


def dot_split(a, b):
    a_high, a_low = high_low(a)
    b_high, b_low = high_low(b)
    return dot(a_high, b_high) + (dot(a_high, b_low) + dot(a_low, b_high))


def call(kernel, out_shape, in_specs, *args, scratch=(), flops=0, vmem=16, out_space=VMEM):
    return pl.pallas_call(
        kernel,
        out_shape=out_shape,
        in_specs=in_specs,
        out_specs=jax.tree.map(lambda _: out_space, out_shape),
        scratch_shapes=scratch,
        compiler_params=pltpu.CompilerParams(vmem_limit_bytes=vmem * 2 ** 20),
        cost_estimate=pl.CostEstimate(flops=flops, bytes_accessed=2 ** 20, transcendentals=0),
    )(*args)


def fetch(sems, *pairs):
    copies = [pltpu.make_async_copy(a, b, sems.at[i]) for i, (a, b) in enumerate(pairs)]
    for copy in copies:
        copy.start()
    return copies


def half_kernel(blocks, out, sems):
    half = out.shape[0]
    core = lax.rem(lax.axis_index("tm"), 2)
    fetch(sems, (blocks.at[pl.ds(core * half, half)], out))[0].wait()


def pack_kernel(coarse, neighbours, initial, forcing, small, half, first, force, held, slots, sems):
    copies = fetch(
        sems, (initial, held), (neighbours, slots), (coarse, small.at[pl.ds(0, coarse.shape[0])]),
        (forcing.at[pl.ds(0, force.shape[0])], force),
    )
    for copy in copies[:3]:
        copy.wait()
    small[coarse.shape[0]:, :slots.shape[1]] = slots[...].astype(f32)
    rounded = held[...].astype(bf16).reshape(half.shape)
    half[...] = rounded
    mine = jnp.where(lax.axis_index("tm") == 0, 1.0, 0.0).astype(f32)
    first[...] = (rounded.astype(f32) * mine).astype(bf16)
    copies[3].wait()


def prepare_kernel(
    nbr_in, modes_in, forcing, blocks, tall, both, late, off, diag, last, own, modes, nbr, masks, sems
):
    copies = fetch(
        sems, (blocks, own), (forcing.at[pl.ds(STEPS - 2, 2)], last), (modes_in, modes), (nbr_in, nbr)
    )
    set_masks(masks)
    off[...] = jnp.zeros_like(off)
    diag[...] = jnp.zeros_like(diag)
    copies[2].wait()
    rows, size = tall.shape[0], tall.shape[1] // 2
    bricks = size // Q
    r = modes[...]
    lane = lax.broadcasted_iota(jnp.int32, (Q, size), 1)
    row = lax.broadcasted_iota(jnp.int32, (Q, size), 0)
    pick = (lane % Q == row).astype(f32)
    spread = lax.dot_general(
        r, pick, (((0,), (0,)), ((), ())), preferred_element_type=f32, precision=highest
    )
    owner = lax.broadcasted_iota(jnp.int32, (BRICK, size), 1) // Q
    for b in range(bricks):
        high, low = high_low(jnp.where(owner == b, spread, 0.0))
        tall[pl.ds(b * BRICK, BRICK), :size] = high
        tall[pl.ds(b * BRICK, BRICK), size:] = low
    gram = lax.dot_general(
        r, r, (((1,), (1,)), ((), ())), preferred_element_type=f32, precision=highest
    )
    rest = r - dot_f32(gram, r)
    for at, value in enumerate((r, rest)):
        pair = jnp.concatenate([value, value], axis=1)
        stack = jnp.concatenate([pair] * bricks, axis=0)
        mine = lax.broadcasted_iota(jnp.int32, stack.shape, 0) // Q
        half = lax.broadcasted_iota(jnp.int32, stack.shape, 1) // BRICK
        for t in range(rows // 128):
            both[pl.ds(at * size, size), pl.ds(t * 128, 128)] = jnp.where(
                mine == 2 * t + half, stack, 0.0
            ).astype(bf16)
    copies[0].wait()
    copies[3].wait()
    here = own.shape[0]
    first_brick = lax.axis_index("space") * here
    for b in range(here):
        place_brick(own, b, nbr, b, first_brick, bricks, b, b % GROUP, off, diag, masks)
    copies[1].wait()
    rows_here = here * BRICK
    count = here * Q
    late[:rows_here, :] = last[0].reshape(rows_here, last.shape[3])
    value = last[1].reshape(rows_here, last.shape[3])
    for at in range(2):
        late[pl.ds(rows_here + at * count, count), :] = dot(
            both[pl.ds(at * size, count), :rows_here], value
        ).astype(bf16)


def place_brick(source, r, nbr, b, first_brick, bricks, row, in_group, off, diag, masks):
    start = row * BRICK if isinstance(row, int) else pl.multiple_of(row * BRICK, BRICK)
    slots = source.shape[2] // BRICK
    for s in range(slots):
        width = min(128, source.shape[2] - (s // 2) * 128)
        tile = source[r, :, pl.ds((s // 2) * 128, width)]
        tile = tile[:, (s % 2) * BRICK:(s % 2 + 1) * BRICK]
        double = jnp.concatenate([tile, tile], axis=1)
        if s == 0:
            diag[pl.ds(start, BRICK), pl.ds((in_group // 2) * 128, 128)] = (
                double * masks[in_group % 2]
            )
        else:
            place = lax.rem(nbr[b, s - 1] - first_brick + bricks, bricks)
            at = lax.div(place, 2)
            off[at, pl.ds(start, BRICK), :] += double * masks[lax.rem(place, 2)]


def set_masks(masks):
    lane = lax.broadcasted_iota(jnp.int32, (BRICK, 128), 1)
    masks[0] = (lane < BRICK).astype(f32).astype(bf16)
    masks[1] = (lane >= BRICK).astype(f32).astype(bf16)


def operator_kernel(parts, nbr, own_off, own_diag, *refs):
    count = 2 * (parts - 1)
    pieces = refs[:count]
    first = refs[count]
    far_first = refs[count + 1:count + parts]
    tall, phi, state, far_off, far_diag, lin, left, masks = refs[count + parts:]
    own = own_diag.shape[0]
    here = own // BRICK
    bricks = here * parts
    groups = bricks // GROUP
    span = GROUP * BRICK
    set_masks(masks)
    far_off[...] = jnp.zeros_like(far_off)
    far_diag[...] = jnp.zeros_like(far_diag)
    half = here // 2
    core = lax.rem(lax.axis_index("tm"), 2)
    first_brick = lax.axis_index("space") * here
    for p in range(parts - 1):
        for j in range(half):
            for piece, side in ((0, core), (1, 1 - core)):
                row = here * p + j + half * side
                place_brick(
                    pieces[2 * p + piece], j, nbr, row, first_brick, bricks, row, j % GROUP,
                    far_off, far_diag, masks,
                )

    def near(r, k):
        return (r - k) % groups in (0, 1, groups - 1)

    def off_tile(r, k):
        ref, at = (own_off, r * span) if r * span < own else (far_off, r * span - own)
        return jnp.concatenate(
            [ref[k * (span // 128) + i, pl.ds(at, span), :] for i in range(span // 128)], axis=1
        )

    def diag_tile(r):
        ref, at = (own_diag, r * span) if r * span < own else (far_diag, r * span - own)
        return ref[pl.ds(at, span), :]

    def at(r, k):
        return pl.ds(r * span, span), pl.ds(k * span, span)

    for k in range(groups):
        for r in range(groups):
            if near(r, k):
                lin[at(r, k)] = dot(off_tile(r, k), diag_tile(k)).astype(bf16)
                left[at(r, k)] = dot(diag_tile(r), lin[at(r, k)]).astype(bf16)
    for n in range(groups):
        for r in range(groups):
            out = None
            for k in range(groups):
                if near(r, k) and near(k, n):
                    part = dot(left[at(r, k)], lin[at(k, n)])
                    out = part if out is None else out + part
            if out is None:
                out = jnp.zeros((span, span), f32)
            if near(r, n):
                out = out - left[at(r, n)].astype(f32)
            if r == n:
                out = out + diag_tile(r).astype(f32)
            phi[at(r, n)] = out.astype(bf16)
    begin = jnp.concatenate([first[...]] + [r[...] for r in far_first], axis=0)
    size = tall.shape[1] // 2
    state[...] = dot(phi[...], jnp.concatenate([begin, tall[:, :size]], axis=1))


def advance(parts, full, force, far_force, i, iterates, images):
    own, ens = force.shape[1], force.shape[2]
    mine = full[:own, :ens] + force[i].astype(f32)
    iterates[0] = mine
    moved = full[:, ens:].astype(bf16)
    images[0] = moved[:own]
    rows = [mine.astype(bf16)]
    for p in range(parts - 1):
        far = full[own * (p + 1):own * (p + 2), :ens]
        if far_force is not None:
            far = far + far_force[p].astype(f32)
        rows.append(far.astype(bf16))
    return jnp.concatenate([jnp.concatenate(rows, axis=0), moved], axis=1)


def early_kernel(parts, phi, state, force, *refs):
    far_force = refs[:parts - 1]
    iterates, images, out = refs[parts - 1:]
    own, ens = force.shape[1], force.shape[2]
    full = state[...]
    for i in range(iterates.shape[0]):
        far = [r[i].reshape(own, ens) for r in far_force]
        current = advance(
            parts, full, force, far, i, iterates.at[pl.ds(i, 1)], images.at[pl.ds(i, 1)]
        )
        full = dot(phi[...], current)
    out[...] = full


def late_kernel(parts, phi, state, force, both, *refs):
    far_late = refs[:parts - 1]
    iterates, images, start, sent, coarse_phi = refs[parts - 1:]
    own, ens = force.shape[1], force.shape[2]
    far = [r[:own, :] for r in far_late]
    current = advance(
        parts, state[...], force, far, STEPS - 2, iterates.at[pl.ds(0, 1)], images.at[pl.ds(0, 1)]
    )
    full = dot(phi[...], current)
    current = advance(
        parts, full, force, None, STEPS - 1, iterates.at[pl.ds(1, 1)], images.at[pl.ds(1, 1)]
    )
    got = dot(both[...], current)
    size = got.shape[0] // 2
    each = size // parts
    begin = got[:, :ens] + jnp.concatenate(
        [
            part
            for at in range(2)
            for part in [jnp.zeros((each, ens), f32)]
            + [r[pl.ds(own + at * each, each), :].astype(f32) for r in far_late]
        ],
        axis=0,
    )
    start[...] = begin
    sent[...] = begin.astype(bf16)
    coarse_phi[...] = got[:size, ens:]


def write_powers(out, step, moved):
    wide = step.shape[0]
    for at, value in enumerate((step, moved)):
        high, low = high_low(value)
        out[pl.ds(at * wide, wide), :wide] = high
        out[pl.ds(at * wide, wide), wide:] = low


def unit(wide):
    at = lax.broadcasted_iota(jnp.int32, (wide, wide), 0)
    to = lax.broadcasted_iota(jnp.int32, (wide, wide), 1)
    return (at == to).astype(f32)


def bit_of_place(i):
    return lax.rem(lax.shift_right_logical(lax.axis_index("tm"), i), 2) == 1


def recurrence_kernel(modes, own_coarse, *refs):
    far_coarse = refs[:-3]
    coarse_phi, step_out, out = refs[-3:]
    size = coarse_phi.shape[0]
    lane = lax.broadcasted_iota(jnp.int32, (Q, size), 1)
    row = lax.broadcasted_iota(jnp.int32, (Q, size), 0)
    pick = (lane % Q == row).astype(f32)
    tall = jnp.concatenate([own_coarse[...]] + [r[:own_coarse.shape[0]] for r in far_coarse], axis=0)
    same = (
        lax.broadcasted_iota(jnp.int32, (size, size), 0) // Q
        == lax.broadcasted_iota(jnp.int32, (size, size), 1) // Q
    )
    a = jnp.where(same, dot_f32(tall, pick), 0.0)
    r = modes[...]
    gram = lax.dot_general(
        r, r, (((1,), (1,)), ((), ())), preferred_element_type=f32, precision=highest
    )
    gram = jnp.where(same, jnp.concatenate([dot_f32(gram, pick)] * (size // Q), axis=0), 0.0)
    lower = coarse_phi[...] - dot_split(gram, a)
    step = jnp.concatenate(
        [
            jnp.concatenate([a, jnp.zeros((size, size), f32)], axis=1),
            jnp.concatenate([lower, a], axis=1),
        ],
        axis=0,
    )
    step_out[...] = step
    write_powers(out, step, jnp.where(bit_of_place(0), unit(2 * size), 0.0))


def powers_kernel(bits, step_in, *outs):
    step = step_in[...]
    moved = unit(step.shape[0])
    for i in range(1, bits):
        moved = jnp.where(bit_of_place(i - 1), dot_split(moved, step), moved)
        step = dot_split(step, step)
        write_powers(outs[i - 1], step, jnp.where(bit_of_place(i), moved, 0.0))


def join_kernel(turn, powers, mine, other, *refs):
    total, prefix = refs[-2:]
    wide = mine.shape[0]
    upper = bit_of_place(turn)
    own, came = mine[...].astype(bf16).astype(f32), other[...].astype(f32)
    low = jnp.where(upper, came, own).astype(bf16)
    high = jnp.where(upper, own, came)
    moved = dot(powers[...], jnp.concatenate([low, low], axis=0))
    total[...] = (moved[:wide] + high).astype(bf16)
    if turn == 0:
        prefix[...] = moved[wide:]
    else:
        prefix[...] = refs[0][...] + moved[wide:]


def last_kernel(
    powers, other, before, step, start, tall, early_images, late_images, early, late,
    solution, defect, held, sems
):
    wide = before.shape[0]
    size = wide // 2
    shape = defect.shape

    def send(i, value):
        held[i] = value.reshape(shape)
        to = solution.at[i] if i < STEPS else defect
        copy = pltpu.make_async_copy(held.at[i], to, sems.at[i])
        copy.start()
        return copy

    came = other[...]
    prefix = before[...] + dot(powers[pl.ds(wide, wide), :], jnp.concatenate([came, came], axis=0))
    low = prefix.astype(bf16)
    sum_low = (prefix[:size] + prefix[size:]).astype(bf16)
    images = [early_images[i] for i in range(STEPS - 2)] + [late_images[i] for i in range(2)]
    iterates = [early.at[i] for i in range(STEPS - 2)] + [late.at[i] for i in range(2)]
    copies = [send(i, iterates[i][...] + dot(images[i], sum_low)) for i in range(STEPS - 1)]
    mine = dot(step[pl.ds(0, wide), :], jnp.concatenate([low, low], axis=0)) + start[...]
    first = mine[:size].astype(bf16)
    both = (mine[:size] + mine[size:]).astype(bf16)
    own = early.shape[1]
    m = tall[:own, :]
    copies.append(send(STEPS - 1, dot(m, jnp.concatenate([both, both], axis=0))))
    copies.append(send(
        STEPS,
        iterates[STEPS - 1][...]
        + dot(images[STEPS - 1], low[:size])
        - dot(m, jnp.concatenate([first, first], axis=0)),
    ))
    for copy in copies:
        copy.wait()


def dense_body(initial, forcing, brick_blocks, neighbours, coarse_modes, coarse_blocks):
    here, _, ens = initial.shape
    parts = lax.axis_size("space")
    bricks = here * parts
    own = here * BRICK
    rows = bricks * BRICK
    size = bricks * Q
    slices = lax.axis_size("tm")
    bits = slices.bit_length() - 1
    sds = jax.ShapeDtypeStruct

    def in_hbm(value):
        return pltpu.with_memory_space_constraint(value, pltpu.HBM)

    def others(value):
        return [
            lax.ppermute(value, "space", [((s + k) % parts, s) for s in range(parts)])
            for k in range(1, parts)
        ]

    def paired(value, bit):
        return lax.ppermute(value, "tm", [(j, j ^ (1 << bit)) for j in range(slices)])

    half = here // 2
    coarse = coarse_blocks.reshape(here * Q, Q)
    force = forcing.reshape(STEPS, own, ens)
    slots = neighbours.shape[1]
    some = call(
        half_kernel, sds((half,) + brick_blocks.shape[1:], bf16), [HBM],
        in_hbm(brick_blocks),
        scratch=[pltpu.SemaphoreType.DMA((1,))],
    )
    fetched = others(some)
    small, start_half, first, send_force = call(
        pack_kernel,
        (
            sds((here * Q + here, Q), f32),
            sds((own, ens), bf16),
            sds((own, ens), bf16),
            sds((STEPS - 2,) + forcing.shape[1:], bf16),
        ),
        [HBM] * 4,
        in_hbm(coarse), in_hbm(neighbours), in_hbm(initial), in_hbm(forcing),
        scratch=[
            pltpu.VMEM(initial.shape, f32),
            pltpu.VMEM(neighbours.shape, jnp.int32),
            pltpu.SemaphoreType.DMA((4,)),
        ],
    )
    far_small = others(small)
    far_first = [
        lax.ppermute(
            start_half, ("tm", "space"), [((s + k) % parts, s) for s in range(parts)]
        )
        for k in range(1, parts)
    ]
    far_force = others(send_force)
    tall, both, late, own_off, own_diag = call(
        prepare_kernel,
        (
            sds((rows, 2 * size), bf16),
            sds((2 * size, rows), bf16),
            sds((own + 2 * here * Q, ens), bf16),
            sds((rows // 128, own, 128), bf16),
            sds((own, GROUP * BRICK), bf16),
        ),
        [HBM] * 4,
        in_hbm(neighbours), in_hbm(coarse_modes), in_hbm(forcing), in_hbm(brick_blocks),
        scratch=[
            pltpu.VMEM((2,) + forcing.shape[1:], bf16),
            pltpu.VMEM(brick_blocks.shape, bf16),
            pltpu.VMEM(coarse_modes.shape, f32),
            pltpu.SMEM(neighbours.shape, jnp.int32),
            pltpu.VMEM((2, BRICK, 128), bf16),
            pltpu.SemaphoreType.DMA((4,)),
        ],
    )
    pieces = [piece for f in fetched for piece in (f, paired(f, 0))]
    far_late = others(late)
    far_nbr = [f[here * Q:, :slots].astype(jnp.int32) for f in far_small]
    far_nbr = far_nbr[0] if parts == 2 else jnp.concatenate(far_nbr, axis=0)
    phi, state = call(
        functools.partial(operator_kernel, parts),
        (sds((rows, rows), bf16), sds((rows, ens + size), f32)),
        [SMEM] + [VMEM] * (3 * parts + 1),
        far_nbr, own_off, own_diag, *pieces, first, *far_first, tall,
        scratch=[
            pltpu.VMEM((rows // 128, rows - own, 128), bf16),
            pltpu.VMEM((rows - own, GROUP * BRICK), bf16),
            pltpu.VMEM((rows, rows), bf16),
            pltpu.VMEM((rows, rows), bf16),
            pltpu.VMEM((2, BRICK, 128), bf16),
        ],
        flops=2 * 4 * rows * rows * ens,
        vmem=20,
    )
    early_iterates, early_images, state = call(
        functools.partial(early_kernel, parts),
        (
            sds((STEPS - 2, own, ens), f32),
            sds((STEPS - 2, own, size), bf16),
            sds((rows, ens + size), f32),
        ),
        [VMEM] * (2 + parts),
        phi, state, force, *far_force,
        flops=2 * 2 * rows * rows * (ens + size),
    )
    late_iterates, late_images, start, sent, coarse_phi = call(
        functools.partial(late_kernel, parts),
        (
            sds((2, own, ens), f32),
            sds((2, own, size), bf16),
            sds((2 * size, ens), f32),
            sds((2 * size, ens), bf16),
            sds((size, size), f32),
        ),
        [VMEM] * (3 + parts),
        phi, state, force, both, *far_late,
        flops=2 * rows * rows * (ens + size),
    )
    table = sds((4 * size, 4 * size), bf16)
    step, opening = call(
        recurrence_kernel,
        (sds((2 * size, 2 * size), f32), table),
        [VMEM] * (2 + parts),
        coarse_modes, coarse, *far_small, coarse_phi,
        flops=2 * 3 * (2 * size) ** 3,
    )
    powers = [opening] + list(call(
        functools.partial(powers_kernel, bits),
        (table,) * (bits - 1),
        [VMEM],
        step,
        flops=2 * 18 * (2 * size) ** 3,
    ))
    total = sent
    prefix = None
    for i in range(bits):
        other = paired(total, i)
        if i < bits - 1:
            total, prefix = call(
                functools.partial(join_kernel, i),
                (sds((2 * size, ens), bf16), sds((2 * size, ens), f32)),
                [VMEM] * (3 if prefix is None else 4),
                powers[i], total, other, *(() if prefix is None else (prefix,)),
            )
    solution_out, defect = call(
        last_kernel,
        (sds((STEPS, here, BRICK, ens), f32), sds((here, BRICK, ens), f32)),
        [VMEM] * 10,
        powers[bits - 1], other, prefix, powers[0], start, tall, early_images, late_images,
        early_iterates, late_iterates,
        scratch=[
            pltpu.VMEM((STEPS + 1, here, BRICK, ens), f32),
            pltpu.SemaphoreType.DMA((STEPS + 1,)),
        ],
        out_space=pl.BlockSpec(memory_space=pl.ANY),
    )
    return solution_out, defect[None]


def solution(mesh):
    placed = (
        P("space", None, None),
        P("tm", "space", None, None),
        P("space", None, None),
        P("space", None),
        P(),
        P("space", None, None),
    )

    def body(initial, *rest):
        here = initial.shape[0]
        bricks = here * lax.axis_size("space")
        slices = lax.axis_size("tm")
        fits = 8 * (bricks * BRICK) ** 2 <= 16 * 2 ** 20
        even = here % (2 * GROUP) == 0 and slices > 2 and slices & (slices - 1) == 0
        return (dense_body if fits and even else banded_body)(initial, *rest)

    return jax.shard_map(
        body,
        mesh=mesh,
        in_specs=placed,
        out_specs=(P("tm", "space", None, None), P("tm", "space", None, None)),
        check_vma=False,
    )
```

time: 50.1 us -> 47.7 us (0.952)
  waiting for transfers between devices: 16.3 us -> 21 us
  other arithmetic: 2.52 us -> 0.01 us
  matrix products: 2.13 us -> 0 us
  local copies, waits for them, and re-layouts: 2.14 us -> 0.02 us
  starting transfers between devices: 9.45 us -> 10.1 us
  Pallas kernels: 16.2 us -> 15.6 us
    ppermute x4, waiting for transfers between devices: 0.01 us -> 6.47 us  [others(): lax.ppermute(value, 'space', [((s + k) % parts, s) for s in range(parts)])]
    dot_general x3 -> x0, matrix products: 2.13 us -> none  [the longest x1 1.08 us: dense_body(): jnp.einsum('qc,bce->bqe', coarse_modes, forcing[STEPS - 1].astype(f32), p...]
    ppermute x5, waiting for transfers between devices: 14 us -> 12.8 us  [paired(): return lax.ppermute(value, 'tm', [(j, j ^ 1 << bit) for j in range(slices)])]
    slice x3 -> x0, local copies, waits for them, and re-layouts: 1.05 us -> none  [the longest x1 1.02 us: dense_body(): far_force = others(force[:STEPS - 1])]
    select_n x2 -> x0, other arithmetic: 0.98 us -> none  [the longest x1 0.97 us: dense_body(): first = jnp.where(place == 0, start_half, jnp.zeros_like(start_half))]
    dynamic_slice x1 -> x0, local copies, waits for them, and re-layouts: 0.97 us -> none  [dense_body(): some = lax.dynamic_slice_in_dim(brick_blocks, core * half, half, axis=0)]
    convert_element_type x3 -> x1, other arithmetic: 0.77 us -> 0.01 us  [dense_body(): far_nbr = [f[here * Q:, :slots].astype(jnp.int32) for f in far_small]]
    concatenate x1 -> x0, other arithmetic: 0.76 us -> none  [dense_body(): jnp.concatenate([coarse_blocks.reshape(here * Q, Q), jnp.pad(neighbours.a...]
  transfers between devices with their start and end apart: 10 -> 10, of which waited for: 4 -> 7; matrix products, arithmetic and copies ran while one was open for 11% -> 0% of each run, Pallas kernels for 21% -> 23%
where the time goes in v3:
time: 47.7 us; the launch traced here: 47.5 us
  waiting for transfers between devices  21 us (44%)
  Pallas kernels  15.6 us (33%)
  starting transfers between devices  10.1 us (21%)
  between operations  0.78 us (2%)
    pallas_call x12, Pallas kernels, call(): pl.pallas_call(kernel, out_shape=out_shape, in_specs=in_specs, out_specs=...  15.6 us
    ppermute x5, waiting for transfers between devices, paired(): return lax.ppermute(value, 'tm', [(j, j ^ 1 << bit) for j in range(slices)])  12.8 us
    ppermute x4, starting transfers between devices, others(): lax.ppermute(value, 'space', [((s + k) % parts, s) for s in range(parts)])  7.01 us
    ppermute x4, waiting for transfers between devices, others(): lax.ppermute(value, 'space', [((s + k) % parts, s) for s in range(parts)])  6.47 us
    ppermute x1, starting transfers between devices, dense_body(): lax.ppermute(start_half, ('tm', 'space'), [((s + k) % parts, s) for s in...  2.18 us
    ppermute x1, waiting for transfers between devices, dense_body(): lax.ppermute(start_half, ('tm', 'space'), [((s + k) % parts, s) for s in...  1.75 us
  transfers between devices with their start and end apart: 10, of which 7 were waited for; matrix products, arithmetic and copies ran while one was open for 0% of the time, Pallas kernels for 23%

profile of v3, /device:TPU:0, one launch (start us, length us, event | category | flops | bytes accessed | tf_op | source)
XLA Modules:
  0.0 47.5 jit_solution(6649014251103905891)
XLA Ops:
  0.6 1.0 %shard_map.79 = bf16[4,64,448]{2,1,0:T(8,128)(2,1)S(1)} custom-call(bf16[8,64,448]{2,1,0:T(8,128)(2,1)} %blocks.3), custom_call_target="tpu_custom_call" | custom-call | bytes 1048576 | tf_op jit(solution)/shard_map/pallas_call | solution.py:154
  1.6 3.1 %collective-permute-start.1 = (bf16[4,64,448]{2,1,0:T(8,128)(2,1)S(1)}, bf16[4,64,448]{2,1,0:T(8,128)(2,1)S(1)}, u32[]{:S(2)}, u32[]{:S(2)}) collective-permute-start(bf16[4,64,448]{2,1,0:T(8,128)(2,1)S(1)} %shard_map.79), channel_id=1, source_target_pairs={{1,0},{0,1},{3,2},{2,3},{5,4},{4,5},{7,6},{6,7},{9,8},{8,9},{11,10... | collective-permute-start | bytes 688136 | tf_op jit(solution)/shard_map/ppermute | solution.py:521
  4.7 6.3 %collective-permute-done.1.refs_0_ = bf16[4,64,448]{2,1,0:T(8,128)(2,1)S(1)} collective-permute-done((bf16[4,64,448]{2,1,0:T(8,128)(2,1)S(1)}, bf16[4,64,448]{2,1,0:T(8,128)(2,1)S(1)}, u32[]{:S(2)}, u32[]{:S(2)}) %collective-permute-start.1) | collective-permute-done | bytes 229408 | tf_op jit(solution)/shard_map/ppermute | solution.py:521
  11.0 0.0 collective-permute-start.2
  11.0 1.1 %shard_map.77 = (f32[72,8]{1,0:T(8,128)S(1)}, bf16[512,128]{1,0:T(8,128)(2,1)S(1)}, bf16[512,128]{1,0:T(8,128)(2,1)S(1)}, bf16[2,8,64,128]{3,2,1,0:T(8,128)(2,1)S(1)}) custom-call(f32[64,8]{1,0:T(8,128)} %bitcast.5, s32[8,6]{1,0:T(8,128)} %nbr_in.1, f32[8,64,128]{2,1,0:T(8,128)} %initial.1, bf16[4,8,64,128]{3,2,1,0:T(8,128)(2,1)} %forcing.3), custom_call_target="tpu_custom_call" | custom-call | bytes 1048576 | tf_op jit(solution)/shard_map/pallas_call | solution.py:154
  12.1 1.8 %collective-permute-start = (f32[72,8]{1,0:T(8,128)S(1)}, f32[72,8]{1,0:T(8,128)S(1)}, u32[]{:S(2)}, u32[]{:S(2)}) collective-permute-start(f32[72,8]{1,0:T(8,128)S(1)} %get-tuple-element.34), channel_id=1, source_target_pairs={{1,0},{0,1},{3,2},{2,3},{5,4},{4,5},{7,6},{6,7},{9,8},{8,9},{11,10... | collective-permute-start | bytes 6920 | tf_op jit(solution)/shard_map/ppermute | solution.py:521
  13.9 2.2 %collective-permute-start.3 = (bf16[512,128]{1,0:T(8,128)(2,1)S(1)}, bf16[512,128]{1,0:T(8,128)(2,1)S(1)}, u32[]{:S(2)}, u32[]{:S(2)}) collective-permute-start(bf16[512,128]{1,0:T(8,128)(2,1)S(1)} %get-tuple-element.38), channel_id=1, source_target_pairs={{1,0},{0,1}} | collective-permute-start | bytes 393224 | tf_op jit(solution)/shard_map/ppermute | solution.py:556
  16.1 1.8 %collective-permute-start.4 = (bf16[2,8,64,128]{3,2,1,0:T(8,128)(2,1)S(1)}, bf16[2,8,64,128]{3,2,1,0:T(8,128)(2,1)S(1)}, u32[]{:S(2)}, u32[]{:S(2)}) collective-permute-start(bf16[2,8,64,128]{3,2,1,0:T(8,128)(2,1)S(1)} %get-tuple-element.42), channel_id=1, source_target_pairs={{1,0},{0,1},{3,2},{2,3},{5,4},{4,5},{7,6},{6,7},{9,8},{8,9},{11,10... | collective-permute-start | bytes 786440 | tf_op jit(solution)/shard_map/ppermute | solution.py:521
  17.9 2.1 %shard_map.78 = (bf16[1024,256]{1,0:T(8,128)(2,1)S(1)}, bf16[256,1024]{1,0:T(8,128)(2,1)S(1)}, bf16[640,128]{1,0:T(8,128)(2,1)S(1)}, bf16[8,512,128]{2,1,0:T(8,128)(2,1)S(1)}, bf16[512,256]{1,0:T(8,128)(2,1)S(1)}) custom-call(s32[8,6]{1,0:T(8,128)} %nbr_in.1, f32[8,64]{1,0:T(8,128)} %modes.1, bf16[4,8,64,128]{3,2,1,0:T(8,128)(2,1)} %forcing.3, ...), custom_call_target="tpu_custom_call" | custom-call | bytes 1048576 | tf_op jit(solution)/shard_map/pallas_call | solution.py:154
  20.0 0.0 copy-start
  20.0 0.3 collective-permute-start.5
  20.4 0.0 collective-permute-done.refs_0_
  20.4 1.8 %collective-permute-done.3.refs_3_ = bf16[512,128]{1,0:T(8,128)(2,1)S(1)} collective-permute-done((bf16[512,128]{1,0:T(8,128)(2,1)S(1)}, bf16[512,128]{1,0:T(8,128)(2,1)S(1)}, u32[]{:S(2)}, u32[]{:S(2)}) %collective-permute-start.3) | collective-permute-done | bytes 131104 | tf_op jit(solution)/shard_map/ppermute | solution.py:556
  22.1 0.0 collective-permute-done.2.refs_1_
  22.1 3.9 %shard_map.80 = (bf16[1024,1024]{1,0:T(8,128)(2,1)S(1)}, f32[1024,256]{1,0:T(8,128)S(1)}) custom-call(s32[8,6]{1,0:T(8,128)S(1)} %slice_convert_fusion.nbr, bf16[8,512,128]{2,1,0:T(8,128)(2,1)S(1)} %get-tuple-element.35.own_off, bf16[512,256]{1,0:T(8,128)(2,1)S(1)} %get-tuple-element.36.own_diag, bf16[4,64,448]{2,1,0:T(8,128)(2,1)S(1)} %collective-permute-done.1.refs_0_, ...), custom_call_target="tpu_custom_call" | custom-call | flops 1073741824 | bytes 1048576 | tf_op jit(solution)/shard_map/pallas_call | solution.py:154
  26.1 0.2 collective-permute-done.4.refs_0_
  26.2 0.0 copy-done
  26.2 2.2 %shard_map.81 = (f32[2,512,128]{2,1,0:T(8,128)S(1)}, bf16[2,512,128]{2,1,0:T(8,128)(2,1)S(1)}, f32[1024,256]{1,0:T(8,128)S(1)}) custom-call(bf16[1024,1024]{1,0:T(8,128)(2,1)S(1)} %get-tuple-element.40.phi, f32[1024,256]{1,0:T(8,128)S(1)} %get-tuple-element.41.state, bf16[4,512,128]{2,1,0:T(8,128)(2,1)S(1)} %bitcast.3, ...), custom_call_target="tpu_custom_call" | custom-call | flops 1073741824 | bytes 1048576 | tf_op jit(solution)/shard_map/pallas_call | solution.py:154
  28.5 0.0 collective-permute-done.5.refs_0_
  28.5 0.0 copy-start.1
  28.5 0.0 copy-start.2
  28.5 1.0 %shard_map.82 = (f32[2,512,128]{2,1,0:T(8,128)S(1)}, bf16[2,512,128]{2,1,0:T(8,128)(2,1)S(1)}, f32[256,128]{1,0:T(8,128)S(1)}, bf16[256,128]{1,0:T(8,128)(2,1)S(1)}, f32[128,128]{1,0:T(8,128)S(1)}) custom-call(bf16[1024,1024]{1,0:T(8,128)(2,1)S(1)} %get-tuple-element.40.phi, f32[1024,256]{1,0:T(8,128)S(1)} %get-tuple-element.43.state, ...), custom_call_target="tpu_custom_call" | custom-call | flops 536870912 | bytes 1048576 | tf_op jit(solution)/shard_map/pallas_call | solution.py:154
  29.5 0.1 collective-permute-start.6
  29.6 0.0 copy-done.1
  29.6 0.0 copy-done.2
  29.6 0.5 %shard_map.83 = (f32[256,256]{1,0:T(8,128)S(1)}, bf16[512,512]{1,0:T(8,128)(2,1)S(1)}) custom-call(f32[8,64]{1,0:T(8,128)S(1)} %copy-done.2, f32[64,8]{1,0:T(8,128)S(1)} %bitcast.6, f32[72,8]{1,0:T(8,128)S(1)} %collective-permute-done.refs_0_, f32[128,128]{1,0:T(8,128)S(1)} %get-tuple-element.46.refs_1_), custom_call_target="tpu_custom_call" | custom-call | flops 100663296 | bytes 1048576 | tf_op jit(solution)/shard_map/pallas_call | solution.py:154
  30.1 0.7 %collective-permute-done.6.other = bf16[256,128]{1,0:T(8,128)(2,1)S(1)} collective-permute-done((bf16[256,128]{1,0:T(8,128)(2,1)S(1)}, bf16[256,128]{1,0:T(8,128)(2,1)S(1)}, u32[]{:S(2)}, u32[]{:S(2)}) %collective-permute-start.6) | collective-permute-done | bytes 65568 | tf_op jit(solution)/shard_map/ppermute | solution.py:526
  30.9 0.3 shard_map.85
  31.1 0.1 collective-permute-start.7
  31.2 1.1 %shard_map.84 = (bf16[512,512]{1,0:T(8,128)(2,1)S(1)}, bf16[512,512]{1,0:T(8,128)(2,1)S(1)}, bf16[512,512]{1,0:T(8,128)(2,1)S(1)}) custom-call(f32[256,256]{1,0:T(8,128)S(1)} %get-tuple-element.47.step_in), custom_call_target="tpu_custom_call" | custom-call | flops 603979776 | bytes 1048576 | tf_op jit(solution)/shard_map/pallas_call | solution.py:154
  32.3 3.1 %collective-permute-done.7.other = bf16[256,128]{1,0:T(8,128)(2,1)S(1)} collective-permute-done((bf16[256,128]{1,0:T(8,128)(2,1)S(1)}, bf16[256,128]{1,0:T(8,128)(2,1)S(1)}, u32[]{:S(2)}, u32[]{:S(2)}) %collective-permute-start.7) | collective-permute-done | bytes 65568 | tf_op jit(solution)/shard_map/ppermute | solution.py:526
  35.5 0.3 shard_map.86
  35.8 0.1 collective-permute-start.8
  35.9 4.3 %collective-permute-done.8.other = bf16[256,128]{1,0:T(8,128)(2,1)S(1)} collective-permute-done((bf16[256,128]{1,0:T(8,128)(2,1)S(1)}, bf16[256,128]{1,0:T(8,128)(2,1)S(1)}, u32[]{:S(2)}, u32[]{:S(2)}) %collective-permute-start.8) | collective-permute-done | bytes 65568 | tf_op jit(solution)/shard_map/ppermute | solution.py:526
  40.1 0.3 shard_map.87
  40.4 0.7 %collective-permute-start.9 = (bf16[256,128]{1,0:T(8,128)(2,1)S(1)}, bf16[256,128]{1,0:T(8,128)(2,1)S(1)}, u32[]{:S(2)}, u32[]{:S(2)}) collective-permute-start(bf16[256,128]{1,0:T(8,128)(2,1)S(1)} %get-tuple-element.57), channel_id=1, source_target_pairs={{0,16},{2,18},{4,20},{6,22},{8,24},{10,26},{12,28},{14,30},{16,0},... | collective-permute-start | bytes 196616 | tf_op jit(solution)/shard_map/ppermute | solution.py:526
  41.2 4.6 %collective-permute-done.9.other = bf16[256,128]{1,0:T(8,128)(2,1)S(1)} collective-permute-done((bf16[256,128]{1,0:T(8,128)(2,1)S(1)}, bf16[256,128]{1,0:T(8,128)(2,1)S(1)}, u32[]{:S(2)}, u32[]{:S(2)}) %collective-permute-start.9) | collective-permute-done | bytes 65568 | tf_op jit(solution)/shard_map/ppermute | solution.py:526
  45.8 1.7 %shard_map.88 = (f32[4,8,64,128]{3,2,1,0:T(8,128)}, f32[8,64,128]{2,1,0:T(8,128)}) custom-call(bf16[512,512]{1,0:T(8,128)(2,1)S(1)} %get-tuple-element.48.powers, bf16[256,128]{1,0:T(8,128)(2,1)S(1)} %collective-permute-done.9.other, f32[256,128]{1,0:T(8,128)S(1)} %get-tuple-element.58.before, bf16[512,512]{1,0:T(8,128)(2,1)S(1)} %get-tuple-element.51.powers.step, ...), custom_call_target="tpu_custom_call" | custom-call | bytes 1048576 | tf_op jit(solution)/shard_map/pallas_call | solution.py:154
  (1 shorter events, 0.0 us)
Async XLA Ops:
  1.6 9.4 %collective-permute-start.1 = (bf16[4,64,448]{2,1,0:T(8,128)(2,1)S(1)}, bf16[4,64,448]{2,1,0:T(8,128)(2,1)S(1)}, u32[]{:S(2)}, u32[]{:S(2)}) collective-permute-start(bf16[4,64,448]{2,1,0:T(8,128)(2,1)S(1)} %shard_map.79), channel_id=1, source_target_pairs={{1,0},{0,1},{3,2},{2,3},{5,4},{4,5},{7,6},{6,7},{9,8},{8,9},{11,10... | collective-permute-start | bytes 688136 | tf_op jit(solution)/shard_map/ppermute | solution.py:521
  11.0 11.2 %collective-permute-start.2 = (bf16[4,64,448]{2,1,0:T(8,128)(2,1)S(1)}, bf16[4,64,448]{2,1,0:T(8,128)(2,1)S(1)}, u32[]{:S(2)}, u32[]{:S(2)}) collective-permute-start(bf16[4,64,448]{2,1,0:T(8,128)(2,1)S(1)} %collective-permute-done.1.refs_0_), channel_id=1, source_target_pairs={{0,2},{2,0},{4,6},{6,4},{8,10},{10,8},{12,14},{14,12},{16,18},{18,... | collective-permute-start | bytes 688136 | tf_op jit(solution)/shard_map/ppermute | solution.py:526
  12.1 8.3 %collective-permute-start = (f32[72,8]{1,0:T(8,128)S(1)}, f32[72,8]{1,0:T(8,128)S(1)}, u32[]{:S(2)}, u32[]{:S(2)}) collective-permute-start(f32[72,8]{1,0:T(8,128)S(1)} %get-tuple-element.34), channel_id=1, source_target_pairs={{1,0},{0,1},{3,2},{2,3},{5,4},{4,5},{7,6},{6,7},{9,8},{8,9},{11,10... | collective-permute-start | bytes 6920 | tf_op jit(solution)/shard_map/ppermute | solution.py:521
  13.9 8.3 %collective-permute-start.3 = (bf16[512,128]{1,0:T(8,128)(2,1)S(1)}, bf16[512,128]{1,0:T(8,128)(2,1)S(1)}, u32[]{:S(2)}, u32[]{:S(2)}) collective-permute-start(bf16[512,128]{1,0:T(8,128)(2,1)S(1)} %get-tuple-element.38), channel_id=1, source_target_pairs={{1,0},{0,1}} | collective-permute-start | bytes 393224 | tf_op jit(solution)/shard_map/ppermute | solution.py:556
  16.1 10.1 %collective-permute-start.4 = (bf16[2,8,64,128]{3,2,1,0:T(8,128)(2,1)S(1)}, bf16[2,8,64,128]{3,2,1,0:T(8,128)(2,1)S(1)}, u32[]{:S(2)}, u32[]{:S(2)}) collective-permute-start(bf16[2,8,64,128]{3,2,1,0:T(8,128)(2,1)S(1)} %get-tuple-element.42), channel_id=1, source_target_pairs={{1,0},{0,1},{3,2},{2,3},{5,4},{4,5},{7,6},{6,7},{9,8},{8,9},{11,10... | collective-permute-start | bytes 786440 | tf_op jit(solution)/shard_map/ppermute | solution.py:521
  20.0 6.2 %copy-start = (bf16[4,8,64,128]{3,2,1,0:T(8,128)(2,1)S(1)}, bf16[4,8,64,128]{3,2,1,0:T(8,128)(2,1)}, u32[]{:S(2)}) copy-start(bf16[4,8,64,128]{3,2,1,0:T(8,128)(2,1)} %forcing.3) | copy-start | bytes 1572868
  20.0 8.4 %collective-permute-start.5 = (bf16[640,128]{1,0:T(8,128)(2,1)S(1)}, bf16[640,128]{1,0:T(8,128)(2,1)S(1)}, u32[]{:S(2)}, u32[]{:S(2)}) collective-permute-start(bf16[640,128]{1,0:T(8,128)(2,1)S(1)} %get-tuple-element.45), channel_id=1, source_target_pairs={{1,0},{0,1},{3,2},{2,3},{5,4},{4,5},{7,6},{6,7},{9,8},{8,9},{11,10... | collective-permute-start | bytes 491528 | tf_op jit(solution)/shard_map/ppermute | solution.py:521
  28.5 1.1 %copy-start.1 = (f32[8,8,8]{2,1,0:T(8,128)S(1)}, f32[8,8,8]{2,1,0:T(8,128)}, u32[]{:S(2)}) copy-start(f32[8,8,8]{2,1,0:T(8,128)} %param.11) | copy-start | bytes 6148
  28.5 1.1 %copy-start.2 = (f32[8,64]{1,0:T(8,128)S(1)}, f32[8,64]{1,0:T(8,128)}, u32[]{:S(2)}) copy-start(f32[8,64]{1,0:T(8,128)} %modes.1) | copy-start | bytes 6148
  29.5 1.3 %collective-permute-start.6 = (bf16[256,128]{1,0:T(8,128)(2,1)S(1)}, bf16[256,128]{1,0:T(8,128)(2,1)S(1)}, u32[]{:S(2)}, u32[]{:S(2)}) collective-permute-start(bf16[256,128]{1,0:T(8,128)(2,1)S(1)} %get-tuple-element.52.mine), channel_id=1, source_target_pairs={{0,2},{2,0},{4,6},{6,4},{8,10},{10,8},{12,14},{14,12},{16,18},{18,... | collective-permute-start | bytes 196616 | tf_op jit(solution)/shard_map/ppermute | solution.py:526
  31.1 4.3 %collective-permute-start.7 = (bf16[256,128]{1,0:T(8,128)(2,1)S(1)}, bf16[256,128]{1,0:T(8,128)(2,1)S(1)}, u32[]{:S(2)}, u32[]{:S(2)}) collective-permute-start(bf16[256,128]{1,0:T(8,128)(2,1)S(1)} %get-tuple-element.53.mine), channel_id=1, source_target_pairs={{0,4},{2,6},{4,0},{6,2},{8,12},{10,14},{12,8},{14,10},{16,20},{18,... | collective-permute-start | bytes 196616 | tf_op jit(solution)/shard_map/ppermute | solution.py:526
  35.8 4.3 %collective-permute-start.8 = (bf16[256,128]{1,0:T(8,128)(2,1)S(1)}, bf16[256,128]{1,0:T(8,128)(2,1)S(1)}, u32[]{:S(2)}, u32[]{:S(2)}) collective-permute-start(bf16[256,128]{1,0:T(8,128)(2,1)S(1)} %get-tuple-element.55.mine), channel_id=1, source_target_pairs={{0,8},{2,10},{4,12},{6,14},{8,0},{10,2},{12,4},{14,6},{16,24},{18,... | collective-permute-start | bytes 196616 | tf_op jit(solution)/shard_map/ppermute | solution.py:526
  40.4 5.4 %collective-permute-start.9 = (bf16[256,128]{1,0:T(8,128)(2,1)S(1)}, bf16[256,128]{1,0:T(8,128)(2,1)S(1)}, u32[]{:S(2)}, u32[]{:S(2)}) collective-permute-start(bf16[256,128]{1,0:T(8,128)(2,1)S(1)} %get-tuple-element.57), channel_id=1, source_target_pairs={{0,16},{2,18},{4,20},{6,22},{8,24},{10,26},{12,28},{14,30},{16,0},... | collective-permute-start | bytes 196616 | tf_op jit(solution)/shard_map/ppermute | solution.py:526
